TPU v7x, 512 devices: a whole 4x4x16 slice. The times are simulated.
512 devices in a mesh: dp: 32 (over x, z_hi, core), space: 16 (over y, z_lo).
Axes of the slice: x: 4, y: 4, z: 16 (z_hi: 4, z_lo: 4; z = z_hi * 4 + z_lo), core: 2. Of those that a mesh axis runs over, the one named last changes fastest.
Arguments:
- field: bfloat16 [32, 64, 32, 16, 128], P('dp', 'space'), may hold values from -6 to 6
- cotangent: bfloat16 [32, 64, 32, 16, 128], P('dp', 'space'), may hold values from -6 to 6
- weights: float32 [16, 128, 2, 128, 128], P('space', 'dp'), may hold values from -0.375 to 0.375
- first_moment: float32 [16, 128, 2, 128, 128], P('space', 'dp'), may hold values from -6 to 6
- second_moment: float32 [16, 128, 2, 128, 128], P('space', 'dp'), may hold values from 0.01 to 10
Outputs:
- field_grad: bfloat16 [32, 64, 32, 16, 128], P('dp', 'space')
- new_weights: float32 [16, 128, 2, 128, 128], P('space', 'dp')
- new_first: float32 [16, 128, 2, 128, 128], P('space', 'dp')
- new_second: float32 [16, 128, 2, 128, 128], P('space', 'dp')
All inputs are finite; a program needn't handle non-finite values.
Results may differ from a plain program's by a relative error of at most 0.024.
Values may be sent and summed in bfloat16 or wider, within the bound.
A program may use at most 64 MiB of HBM per device.

v0:
```python
import math

import jax
import jax.numpy as jnp
from jax import lax
from jax.sharding import PartitionSpec as P

C = 128
MX = 16
MY = 16
MZ = 8
NY = 32
NZ = 16
STEP = 100
MYZ = 128


decay_first = 0.9
decay_second = 0.999
learn_rate = 0.001
adam_floor = 1e-08


def sent_together(arrays, axis, split_dim, concat_dim, along):
    both = jnp.concatenate(arrays, axis=along)
    out, at, outs = (
        lax.all_to_all(both, axis, split_axis=split_dim, concat_axis=concat_dim, tiled=True),
        0,
        [],
    )
    for a in arrays:
        outs.append(lax.slice_in_dim(out, at, at + a.shape[along], axis=along))
        at += a.shape[along]
    return tuple(outs)


def trig_tables(length, modes_kept, signed):
    points = jnp.arange(length, dtype=jnp.int32)
    frequency = jnp.arange(modes_kept, dtype=jnp.int32) - (modes_kept // 2 if signed else 0)
    phases = jnp.mod(points[:, None] * frequency[None, :], length).astype(jnp.float32)
    angles = phases * (2.0 * math.pi / length)
    factor = 1.0 / math.sqrt(length)
    return (
        (jnp.cos(angles) * factor).astype(jnp.bfloat16),
        (jnp.sin(angles) * factor).astype(jnp.bfloat16),
    )


def forward_table(cosine, sine_part):
    real_row = jnp.stack([cosine, -sine_part], axis=-1)
    imag_row = jnp.stack([sine_part, cosine], axis=-1)
    return jnp.stack([real_row, imag_row], axis=1)


def inverse_table(cosine, sine_part):
    real_row = jnp.stack([cosine.T, sine_part.T], axis=-1)
    imag_row = jnp.stack([-sine_part.T, cosine.T], axis=-1)
    return jnp.stack([real_row, imag_row], axis=1)


def adam_update(weights, first_moment, second_moment, weight_grads):
    new_first = decay_first * first_moment + (1.0 - decay_first) * weight_grads
    new_second = decay_second * second_moment + (1.0 - decay_second) * weight_grads * weight_grads
    first_hat = new_first / (1.0 - decay_first**STEP)
    second_hat = new_second / (1.0 - decay_second**STEP)
    new_weights = weights - learn_rate * first_hat / (jnp.sqrt(second_hat) + adam_floor)
    return (new_weights, new_first, new_second)


def on_device(field, cotangent, weights, first_moment, second_moment):
    f32 = jnp.float32
    half = jnp.bfloat16
    slab_count = lax.axis_size("space")
    batch_local = field.shape[0]
    cells_x = field.shape[1]
    total_x = cells_x * slab_count
    cos_z, sin_z = trig_tables(NZ, MZ, False)
    cos_y, sin_y = trig_tables(NY, MY, True)
    cos_x, sin_x = trig_tables(total_x, MX, True)
    table_z = jnp.stack([cos_z, -sin_z], axis=1)
    table_y = forward_table(cos_y, sin_y)
    table_x = forward_table(cos_x, sin_x)
    back_table_x = inverse_table(cos_x, sin_x)
    back_table_y = inverse_table(cos_y, sin_y)
    back_table_z = jnp.stack([cos_z.T, -sin_z.T], axis=0)

    def yz_modes(slab_field):
        first_pass = jnp.einsum(
            "bxyzc,zpk->bxypkc", slab_field, table_z, preferred_element_type=f32
        ).astype(half)
        second = jnp.einsum(
            "bxypkc,ypmq->bxmkqc", first_pass, table_y, preferred_element_type=f32
        ).astype(half)
        return second.reshape(batch_local, cells_x, MYZ, 2, C)

    field_yz = yz_modes(field)
    cot_yz = yz_modes(cotangent)
    field_x, cot_x = sent_together((field_yz, cot_yz), "space", 2, 1, 0)

    def along_x(slab_block):
        return jnp.einsum(
            "bxpjc,xjmq->bmpqc", slab_block, table_x, preferred_element_type=f32
        ).astype(half)

    field_hat, cot_hat = (
        lax.all_to_all(
            lax.all_to_all(along_x(field_x), "space", split_axis=1, concat_axis=2, tiled=True),
            "dp",
            split_axis=2,
            concat_axis=0,
            tiled=True,
        ),
        lax.all_to_all(
            lax.all_to_all(along_x(cot_x), "space", split_axis=1, concat_axis=2, tiled=True),
            "dp",
            split_axis=2,
            concat_axis=0,
            tiled=True,
        ),
    )
    order_in = "bmpj"
    rotated = jnp.stack([cot_hat[:, :, :, 1], -cot_hat[:, :, :, 0]], axis=3)
    form_in = order_in + "c," + order_in + "o->mpco"
    grad_real = jnp.einsum(form_in, field_hat, cot_hat, preferred_element_type=f32)
    grad_imag = jnp.einsum(form_in, field_hat, rotated, preferred_element_type=f32)
    weight_grads = jnp.stack([grad_real, grad_imag], axis=2)
    half_weights = weights.astype(half)
    form_back = "mpjio," + order_in + "o->bmpi"
    back_real = jnp.einsum(form_back, half_weights, cot_hat, preferred_element_type=f32)
    back_imag = jnp.einsum(form_back, half_weights, rotated, preferred_element_type=f32)
    mode_grads = jnp.stack([back_real, back_imag], axis=3).astype(half)
    new_weights, new_first, new_second = adam_update(
        weights, first_moment, second_moment, weight_grads
    )
    pencils = lax.all_to_all(
        lax.all_to_all(mode_grads, "dp", split_axis=0, concat_axis=2, tiled=True),
        "space",
        split_axis=2,
        concat_axis=1,
        tiled=True,
    )
    back_x = jnp.einsum(
        "bmpjc,mjxq->bxpqc", pencils, back_table_x, preferred_element_type=f32
    ).astype(half)
    slab_modes = lax.all_to_all(back_x, "space", split_axis=1, concat_axis=2, tiled=True)
    unpacked = slab_modes.reshape(batch_local, cells_x, MY, MZ, 2, C)
    back_y = jnp.einsum(
        "bxmkjc,mjyq->bxyqkc", unpacked, back_table_y, preferred_element_type=f32
    ).astype(half)
    field_grad = jnp.einsum(
        "bxyqkc,qkz->bxyzc", back_y, back_table_z, preferred_element_type=f32
    ).astype(half)
    return (field_grad, new_weights, new_first, new_second)


def solution(mesh):
    placed = (
        P("dp", "space", None, None, None),
        P("dp", "space", None, None, None),
        P("space", "dp", None, None, None),
        P("space", "dp", None, None, None),
        P("space", "dp", None, None, None),
    )
    return jax.shard_map(
        on_device,
        mesh=mesh,
        in_specs=placed,
        out_specs=(
            P("dp", "space", None, None, None),
            P("space", "dp", None, None, None),
            P("space", "dp", None, None, None),
            P("space", "dp", None, None, None),
        ),
        check_vma=False,
    )
```

profile of v0, /device:TPU:1, one launch (start us, length us, event | category | flops | bytes accessed | tf_op | source)
XLA Modules:
  0.0 151.4 jit_solution(14894665892624491172)
XLA Ops:
  0.6 0.0 copy-start
  0.7 0.1 fusion.84
  0.7 0.1 multiply_convert_fusion.9
  0.8 0.1 fusion.88
  0.9 0.1 multiply_convert_fusion
  1.0 0.6 copy-done
  1.7 0.0 copy-start.4
  1.7 0.3 fusion.3
  2.0 0.8 copy-done.4
  2.7 0.3 fusion.2
  3.0 0.3 fusion.9
  3.3 0.3 fusion.10
  3.6 0.1 copy_bitcast_fusion.1
  3.7 0.1 pad_maximum_fusion
  3.8 1.3 copy.99
  5.1 9.2 %all-to-all-start = ((bf16[2,4,128,2,128]{4,3,1,0,2:T(2,128)(2,1)}), bf16[2,4,128,2,128]{4,3,1,0,2:T(2,128)(2,1)S(1)}, u32[]{:S(2)}, u32[]{:S(2)}) async-start(bf16[2,4,128,2,128]{4,3,1,0,2:T(2,128)(2,1)} %copy.99), calls=%async_computation | async-start | bytes 1048576 | tf_op jit(solution)/shard_map/all_to_all | solution.py:27
  14.3 0.1 fusion.87
  14.4 0.1 multiply_convert_fusion.2
  14.6 15.5 %all-to-all-done = bf16[2,4,128,2,128]{4,3,1,0,2:T(2,128)(2,1)S(1)} async-done(((bf16[2,4,128,2,128]{4,3,1,0,2:T(2,128)(2,1)}), bf16[2,4,128,2,128]{4,3,1,0,2:T(2,128)(2,1)S(1)}, u32[]{:S(2)}, u32[]{:S(2)}) %all-to-all-start) | async-done | bytes 524320 | tf_op jit(solution)/shard_map/all_to_all | solution.py:27
  30.1 0.1 copy.194
  30.3 0.2 copy.101
  30.5 0.2 fusion.15
  30.7 0.0 copy-start.1
  30.7 10.4 %all_to_all.96 = bf16[1,16,8,2,128]{4,2,3,0,1:T(8,128)(2,1)S(1)} all-to-all(bf16[1,16,8,2,128]{4,2,3,0,1:T(8,128)(2,1)S(1)} %copy.102), channel_id=1, replica_groups=mesh['dp'=32,'space'=16] {'space'}, dimensions={1} | all-to-all | bytes 131072 | tf_op jit(solution)/shard_map/all_to_all | solution.py:114
  41.1 0.1 copy.104
  41.2 31.8 %all_to_all.97 = bf16[1,1,128,2,128]{4,3,1,0,2:T(2,128)(2,1)S(1)} all-to-all(bf16[1,1,128,2,128]{4,3,1,0,2:T(2,128)(2,1)S(1)} %copy.104), channel_id=1, replica_groups=mesh['dp'=32,'space'=16] {'dp'}, dimensions={2} | all-to-all | bytes 131072 | tf_op jit(solution)/shard_map/all_to_all | solution.py:113
  73.1 0.0 copy-done.1
  73.1 0.2 fusion.19
  73.3 0.2 fusion.18
  73.6 0.7 copy.110
  74.2 4.3 %all-to-all-start.3 = ((bf16[32,1,4,2,128]{4,2,3,1,0:T(4,128)(2,1)}), bf16[32,1,4,2,128]{4,2,3,1,0:T(4,128)(2,1)S(1)}, u32[]{:S(2)}, u32[]{:S(2)}) async-start(bf16[32,1,4,2,128]{4,2,3,1,0:T(4,128)(2,1)} %copy.110), calls=%async_computation.3 | async-start | bytes 131072 | tf_op jit(solution)/shard_map/all_to_all | solution.py:136
  78.6 0.2 copy.119
  78.8 0.2 fusion.14
  79.0 0.7 copy.120
  79.6 13.7 %all-to-all-done.3 = bf16[32,1,4,2,128]{4,2,3,1,0:T(4,128)(2,1)S(1)} async-done(((bf16[32,1,4,2,128]{4,2,3,1,0:T(4,128)(2,1)}), bf16[32,1,4,2,128]{4,2,3,1,0:T(4,128)(2,1)S(1)}, u32[]{:S(2)}, u32[]{:S(2)}) %all-to-all-start.3) | async-done | bytes 65568 | tf_op jit(solution)/shard_map/all_to_all | solution.py:136
  93.4 3.6 %all-to-all-start.6 = ((bf16[1,16,8,2,128]{4,2,3,0,1:T(8,128)(2,1)}), bf16[1,16,8,2,128]{4,2,3,0,1:T(8,128)(2,1)S(1)}, u32[]{:S(2)}, u32[]{:S(2)}) async-start(bf16[1,16,8,2,128]{4,2,3,0,1:T(8,128)(2,1)} %copy.120), calls=%async_computation.6 | async-start | bytes 131072 | tf_op jit(solution)/shard_map/all_to_all | solution.py:107
  97.0 0.1 fusion.85
  97.1 0.7 copy.112
  97.8 6.1 %all-to-all-done.6 = bf16[1,16,8,2,128]{4,2,3,0,1:T(8,128)(2,1)S(1)} async-done(((bf16[1,16,8,2,128]{4,2,3,0,1:T(8,128)(2,1)}), bf16[1,16,8,2,128]{4,2,3,0,1:T(8,128)(2,1)S(1)}, u32[]{:S(2)}, u32[]{:S(2)}) %all-to-all-start.6) | async-done | bytes 65568 | tf_op jit(solution)/shard_map/all_to_all | solution.py:107
  103.9 3.5 %all-to-all-start.4 = ((bf16[1,1,128,2,128]{4,3,1,0,2:T(2,128)(2,1)}), bf16[1,1,128,2,128]{4,3,1,0,2:T(2,128)(2,1)S(1)}, u32[]{:S(2)}, u32[]{:S(2)}) async-start(bf16[1,1,128,2,128]{4,3,1,0,2:T(2,128)(2,1)} %copy.112), calls=%async_computation.4 | async-start | bytes 131072 | tf_op jit(solution)/shard_map/all_to_all | solution.py:135
  107.5 0.1 fusion.86
  107.6 0.1 multiply_convert_fusion.4
  107.7 0.7 copy.122
  108.4 6.0 %all-to-all-done.4 = bf16[1,1,128,2,128]{4,3,1,0,2:T(2,128)(2,1)S(1)} async-done(((bf16[1,1,128,2,128]{4,3,1,0,2:T(2,128)(2,1)}), bf16[1,1,128,2,128]{4,3,1,0,2:T(2,128)(2,1)S(1)}, u32[]{:S(2)}, u32[]{:S(2)}) %all-to-all-start.4) | async-done | bytes 65568 | tf_op jit(solution)/shard_map/all_to_all | solution.py:135
  114.4 6.4 %all-to-all-start.7 = ((bf16[1,1,128,2,128]{4,3,1,0,2:T(2,128)(2,1)}), bf16[1,1,128,2,128]{4,3,1,0,2:T(2,128)(2,1)S(1)}, u32[]{:S(2)}, u32[]{:S(2)}) async-start(bf16[1,1,128,2,128]{4,3,1,0,2:T(2,128)(2,1)} %copy.122), calls=%async_computation.7 | async-start | bytes 131072 | tf_op jit(solution)/shard_map/all_to_all | solution.py:106
  120.9 0.1 fusion.83
  120.9 0.3 fusion.11
  121.2 0.9 copy.115
  122.1 13.5 %all-to-all-done.7 = bf16[1,1,128,2,128]{4,3,1,0,2:T(2,128)(2,1)S(1)} async-done(((bf16[1,1,128,2,128]{4,3,1,0,2:T(2,128)(2,1)}), bf16[1,1,128,2,128]{4,3,1,0,2:T(2,128)(2,1)S(1)}, u32[]{:S(2)}, u32[]{:S(2)}) %all-to-all-start.7) | async-done | bytes 65568 | tf_op jit(solution)/shard_map/all_to_all | solution.py:106
  135.5 4.0 %all-to-all-start.5 = ((bf16[1,64,8,2,128]{4,2,3,0,1:T(8,128)(2,1)}), bf16[1,64,8,2,128]{4,2,3,0,1:T(8,128)(2,1)S(1)}, u32[]{:S(2)}, u32[]{:S(2)}) async-start(bf16[1,64,8,2,128]{4,2,3,0,1:T(8,128)(2,1)} %copy.115), calls=%async_computation.5 | async-start | bytes 524288 | tf_op jit(solution)/shard_map/all_to_all | solution.py:145
  139.5 0.0 copy-start.2
  139.5 0.1 multiply_convert_fusion.11
  139.6 0.1 multiply_convert_fusion.6
  139.7 0.2 convolution_bitcast_fusion.5
  140.0 0.2 convolution_bitcast_fusion.6
  140.2 0.0 copy-done.3
  140.2 0.3 copy-done.2
  140.5 0.4 copy_subtract_fusion
  140.9 0.8 copy.129
  141.8 0.8 copy.130
  142.6 0.8 copy.131
  143.4 6.5 %all-to-all-done.5 = bf16[1,64,8,2,128]{4,2,3,0,1:T(8,128)(2,1)S(1)} async-done(((bf16[1,64,8,2,128]{4,2,3,0,1:T(8,128)(2,1)}), bf16[1,64,8,2,128]{4,2,3,0,1:T(8,128)(2,1)S(1)}, u32[]{:S(2)}, u32[]{:S(2)}) %all-to-all-start.5) | async-done | bytes 262176 | tf_op jit(solution)/shard_map/all_to_all | solution.py:145
  149.9 0.3 fusion.5
  150.3 1.1 fusion.4
  (17 shorter events, 0.2 us)
Async XLA Ops:
  0.6 1.0 copy-start
  1.7 1.0 copy-start.4
  5.1 25.0 %all-to-all-start = ((bf16[2,4,128,2,128]{4,3,1,0,2:T(2,128)(2,1)}), bf16[2,4,128,2,128]{4,3,1,0,2:T(2,128)(2,1)S(1)}, u32[]{:S(2)}, u32[]{:S(2)}) async-start(bf16[2,4,128,2,128]{4,3,1,0,2:T(2,128)(2,1)} %copy.99), calls=%async_computation | async-start | bytes 1048576 | tf_op jit(solution)/shard_map/all_to_all | solution.py:27
  30.7 42.5 %copy-start.1 = (f32[1,4,2,128,128]{4,3,2,1,0:T(8,128)S(1)}, f32[1,4,2,128,128]{4,3,2,1,0:T(8,128)}, u32[]{:S(2)}) copy-start(f32[1,4,2,128,128]{4,3,2,1,0:T(8,128)} %param.7) | copy-start | bytes 1572868
  74.2 19.2 %all-to-all-start.3 = ((bf16[32,1,4,2,128]{4,2,3,1,0:T(4,128)(2,1)}), bf16[32,1,4,2,128]{4,2,3,1,0:T(4,128)(2,1)S(1)}, u32[]{:S(2)}, u32[]{:S(2)}) async-start(bf16[32,1,4,2,128]{4,2,3,1,0:T(4,128)(2,1)} %copy.110), calls=%async_computation.3 | async-start | bytes 131072 | tf_op jit(solution)/shard_map/all_to_all | solution.py:136
  93.4 10.6 %all-to-all-start.6 = ((bf16[1,16,8,2,128]{4,2,3,0,1:T(8,128)(2,1)}), bf16[1,16,8,2,128]{4,2,3,0,1:T(8,128)(2,1)S(1)}, u32[]{:S(2)}, u32[]{:S(2)}) async-start(bf16[1,16,8,2,128]{4,2,3,0,1:T(8,128)(2,1)} %copy.120), calls=%async_computation.6 | async-start | bytes 131072 | tf_op jit(solution)/shard_map/all_to_all | solution.py:107
  103.9 10.5 %all-to-all-start.4 = ((bf16[1,1,128,2,128]{4,3,1,0,2:T(2,128)(2,1)}), bf16[1,1,128,2,128]{4,3,1,0,2:T(2,128)(2,1)S(1)}, u32[]{:S(2)}, u32[]{:S(2)}) async-start(bf16[1,1,128,2,128]{4,3,1,0,2:T(2,128)(2,1)} %copy.112), calls=%async_computation.4 | async-start | bytes 131072 | tf_op jit(solution)/shard_map/all_to_all | solution.py:135
  114.4 21.1 %all-to-all-start.7 = ((bf16[1,1,128,2,128]{4,3,1,0,2:T(2,128)(2,1)}), bf16[1,1,128,2,128]{4,3,1,0,2:T(2,128)(2,1)S(1)}, u32[]{:S(2)}, u32[]{:S(2)}) async-start(bf16[1,1,128,2,128]{4,3,1,0,2:T(2,128)(2,1)} %copy.122), calls=%async_computation.7 | async-start | bytes 131072 | tf_op jit(solution)/shard_map/all_to_all | solution.py:106
  135.5 4.7 %copy-start.3 = (f32[1,4,2,128,128]{4,3,2,1,0:T(8,128)S(1)}, f32[1,4,2,128,128]{4,3,2,1,0:T(8,128)}, u32[]{:S(2)}) copy-start(f32[1,4,2,128,128]{4,3,2,1,0:T(8,128)} %param.9) | copy-start | bytes 1572868
  135.5 14.4 %all-to-all-start.5 = ((bf16[1,64,8,2,128]{4,2,3,0,1:T(8,128)(2,1)}), bf16[1,64,8,2,128]{4,2,3,0,1:T(8,128)(2,1)S(1)}, u32[]{:S(2)}, u32[]{:S(2)}) async-start(bf16[1,64,8,2,128]{4,2,3,0,1:T(8,128)(2,1)} %copy.115), calls=%async_computation.5 | async-start | bytes 524288 | tf_op jit(solution)/shard_map/all_to_all | solution.py:145
  139.5 1.0 copy-start.2
where the time goes:
time: 152 us; the launch traced here: 151 us
  waiting for transfers between devices  61.3 us (40%)
  blocking collectives  42.2 us (28%)
  starting transfers between devices  31 us (20%)
  local copies, waits for them, and re-layouts  10.1 us (7%)
  matrix products  4.07 us (3%)
  other arithmetic  1.76 us (1%)
    all_to_all x1, blocking collectives, on_device(): lax.all_to_all(lax.all_to_all(along_x(cot_x), 'space', split_axis=1, conc...  31.8 us
    all_to_all x1, waiting for transfers between devices, sent_together(): lax.all_to_all(both, axis, split_axis=split_dim, concat_axis=concat_dim,...  15.5 us
    all_to_all x1, waiting for transfers between devices, on_device(): lax.all_to_all(mode_grads, 'dp', split_axis=0, concat_axis=2, tiled=True)  13.7 us
    all_to_all x1, waiting for transfers between devices, on_device(): lax.all_to_all(lax.all_to_all(along_x(field_x), 'space', split_axis=1, co...  13.5 us
    all_to_all x1, blocking collectives, on_device(): lax.all_to_all(along_x(cot_x), 'space', split_axis=1, concat_axis=2, tile...  10.4 us
    all_to_all x1, starting transfers between devices, sent_together(): lax.all_to_all(both, axis, split_axis=split_dim, concat_axis=concat_dim,...  9.17 us
    all_to_all x1, waiting for transfers between devices, on_device(): lax.all_to_all(back_x, 'space', split_axis=1, concat_axis=2, tiled=True)  6.51 us
    all_to_all x1, starting transfers between devices, on_device(): lax.all_to_all(lax.all_to_all(along_x(field_x), 'space', split_axis=1, co...  6.45 us
  transfers between devices with their start and end apart: 6, of which 6 were waited for; matrix products, arithmetic and copies ran while one was open for 5% of the time, Pallas kernels for 0%

commit v1 on v0

v1 whole, which is shorter than its diff:
```python
import functools

import jax
import jax.numpy as jnp
import numpy as np
from jax import lax
from jax.experimental import pallas as pl
from jax.experimental.pallas import tpu as pltpu
from jax.sharding import PartitionSpec as P
import ml_dtypes

C = 128
MX = 16
MY = 16
MZ = 8
NX = 64
NY = 32
NZ = 16
STEP = 100
MYZ = 128

decay_first = 0.9
decay_second = 0.999
learn_rate = 0.001
adam_floor = 1e-08

MESH = pl.DeviceIdType.MESH
BF16 = jnp.bfloat16
F32 = jnp.float32


def trig_tables(length, modes_kept, signed):
    points = np.arange(length)
    frequency = np.arange(modes_kept) - (modes_kept // 2 if signed else 0)
    phases = np.mod(points[:, None] * frequency[None, :], length).astype(np.float32)
    angles = (phases * np.float32(2.0 * np.pi / length)).astype(np.float32)
    factor = np.float32(1.0 / np.sqrt(length))
    cos_t = (np.cos(angles) * factor).astype(ml_dtypes.bfloat16).astype(np.float32)
    sin_t = (np.sin(angles) * factor).astype(ml_dtypes.bfloat16).astype(np.float32)
    return cos_t, sin_t


def complex_rows(re, im):
    return np.stack([np.stack([re, -im], axis=-1), np.stack([im, re], axis=-1)], axis=1)


@functools.cache
def tables():
    cos_z, sin_z = trig_tables(NZ, MZ, False)
    cos_y, sin_y = trig_tables(NY, MY, True)
    cos_x, sin_x = trig_tables(NX, MX, True)
    ez = cos_z - 1j * sin_z
    ey = cos_y - 1j * sin_y
    ex = cos_x - 1j * sin_x
    yz = np.einsum("ym,zk->mkyz", ey, ez)
    yz = np.stack([yz.real, yz.imag], axis=2).reshape(MYZ * 2, NY * NZ)
    zy = np.einsum("ym,zk->yzmk", ey.conj(), ez.conj())
    zy = np.stack([zy.real, -zy.imag], axis=4).reshape(NY * NZ, MYZ * 2)
    eye = np.eye(8)
    fx = complex_rows(ex.T.real, ex.T.imag)
    fx = np.einsum("msxr,pq->mpsxqr", fx, eye).reshape(MX * 16, NX * 16)
    bx = complex_rows(ex.conj().real, ex.conj().imag)
    bx = np.einsum("xsmr,pq->xpsmqr", bx, eye).reshape(NX * 16, MX * 16)
    return tuple(t.astype(ml_dtypes.bfloat16) for t in (yz, fx, bx, zy))


def tri(v):
    return lax.rem(v * (v + 1) // 2, 4)


def dot(a, b):
    return jnp.dot(a, b, preferred_element_type=F32)


def kernel(
    field_hbm,
    cot_hbm,
    w_hbm,
    yz_hbm,
    fx_hbm,
    bx_hbm,
    modes_hbm,
    grads_hbm,
    cot_v,
    field_v,
    w_v,
    yz_v,
    fx_v,
    bx_v,
    half_v,
    send1,
    recv1,
    send2,
    recv2,
    big_g,
    send3,
    recv3,
    send4,
    grads_v,
    in_sem,
    out_sem,
    send_sem,
    recv_sem,
):
    dp = lax.axis_index("dp")
    sp = lax.axis_index("space")
    gx, gz, core = dp // 8, lax.rem(dp // 2, 4), lax.rem(dp, 2)
    sy, sz = sp // 4, lax.rem(sp, 4)
    mine = dp // 2

    def block_of(x, zh, c, s):
        y, zl = s // 4, lax.rem(s, 4)
        bx_ = lax.rem(x + y + 2 * c, 4)
        bz_ = lax.rem(zh + 3 + (1 + 2 * c) * tri(zl), 4)
        return bx_ * 4 + bz_

    def space_of(x, zh, c, q):
        bx_, bz_ = q // 4, lax.rem(q, 4)
        y = lax.rem(bx_ - x - 2 * c + 8, 4)
        zl = tri(lax.rem((1 + 2 * c) * (bz_ - zh + 5), 4))
        return y * 4 + zl

    my_block = block_of(gx, gz, core, sp)
    self_in = my_block == mine

    def load(k, src, dst):
        copy = pltpu.make_async_copy(src, dst, in_sem.at[k])
        copy.start()
        return copy

    loads = [
        load(0, yz_hbm, yz_v),
        load(1, cot_hbm, cot_v),
        load(2, field_hbm, field_v),
        load(3, fx_hbm, fx_v),
        load(4, w_hbm, w_v),
        load(5, bx_hbm, bx_v),
    ]

    barrier = pltpu.get_barrier_semaphore()

    @pl.loop(0, 16)
    def _(k):
        @pl.when(k != sp)
        def _():
            pl.semaphore_signal(barrier, inc=1, device_id=(dp, k), device_id_type=MESH)

    @pl.loop(0, 32)
    def _(b):
        s = space_of(b // 8, lax.rem(b // 2, 4), lax.rem(b, 2), mine)

        @pl.when(jnp.logical_not(jnp.logical_and(b == dp, s == sp)))
        def _():
            pl.semaphore_signal(barrier, inc=1, device_id=(b, s), device_id_type=MESH)

        there = (2 * my_block + lax.rem(b, 2), b // 2)

        @pl.when(jnp.logical_not(jnp.logical_and(there[0] == dp, there[1] == sp)))
        def _():
            pl.semaphore_signal(barrier, inc=1, device_id=there, device_id_type=MESH)

    def copy_to(src, dst, stage, device):
        same = jnp.logical_and(device[0] == dp, device[1] == sp)

        @pl.when(same)
        def _():
            pltpu.make_async_copy(src, dst, recv_sem.at[stage]).start()

        @pl.when(jnp.logical_not(same))
        def _():
            pltpu.make_async_remote_copy(
                src_ref=src,
                dst_ref=dst,
                send_sem=send_sem.at[stage],
                recv_sem=recv_sem.at[stage],
                device_id=device,
                device_id_type=MESH,
            ).start()

    def yz_modes(k, slab):
        for x in range(4):
            out = dot(yz_v[...], slab[x])
            send1[k, :, x] = out.astype(BF16).reshape(16, 16, C)

    def send_slab(k):
        @pl.loop(0, 16)
        def _(q):
            there = (dp, space_of(gx, gz, core, q))
            copy_to(send1.at[k, q], recv1.at[k, sp], k, there)

    def arrived(buf, stage):
        pltpu.make_async_copy(buf, buf, recv_sem.at[stage]).wait()

    def x_modes(k):
        out = dot(fx_v[...], recv1[k].reshape(1024, C))
        send2[k] = out.astype(BF16).reshape(32, 8, C)

        @pl.loop(0, 32)
        def _(m):
            there = (2 * my_block + lax.rem(m, 2), m // 2)
            copy_to(send2.at[k, m], recv2.at[k, dp], 2 + k, there)

    loads[0].wait()
    loads[1].wait()
    yz_modes(0, cot_v)

    @pl.when(self_in)
    def _():
        pl.semaphore_wait(barrier, 15 + 62)

    @pl.when(jnp.logical_not(self_in))
    def _():
        pl.semaphore_wait(barrier, 15 + 64)

    send_slab(0)
    loads[2].wait()
    yz_modes(1, field_v)
    send_slab(1)
    loads[3].wait()
    loads[4].wait()
    half_v[...] = w_v[...].astype(BF16)

    arrived(recv1.at[0], 0)
    x_modes(0)
    arrived(recv1.at[1], 1)
    x_modes(1)

    arrived(recv2.at[0], 2)
    cot = recv2[0].astype(F32).reshape(256, C)
    row = lax.broadcasted_iota(jnp.int32, (256, C), 0)
    turned = jnp.where(
        lax.rem(row, 2) == 0, pltpu.roll(cot, 255, 0), -pltpu.roll(cot, 1, 0)
    )
    pencil = lax.rem(row // 2, 4)
    back = jnp.zeros((256, C), F32)
    for j in range(4):
        for part, rows in ((0, cot), (1, turned)):
            g = jnp.where(pencil == j, rows, 0.0).astype(BF16)
            big_g[:, pl.ds((2 * j + part) * C, C)] = g
            back += lax.dot_general(
                g, half_v[2 * j + part], (((1,), (1,)), ((), ())), preferred_element_type=F32
            )
    send3[...] = back.astype(BF16).reshape(32, 8, C)

    @pl.loop(0, 32)
    def _(b):
        there = (b, space_of(b // 8, lax.rem(b // 2, 4), lax.rem(b, 2), mine))
        copy_to(send3.at[b], recv3.at[sp, core], 4, there)

    arrived(recv2.at[1], 3)
    left = recv2[1].astype(F32).reshape(256, C).T.astype(BF16)
    for n in range(8):
        grads_v[n] = dot(left, big_g[:, pl.ds(n * C, C)])
    out = pltpu.make_async_copy(grads_v, grads_hbm, out_sem)
    out.start()

    loads[5].wait()
    arrived(recv3, 4)
    out4 = dot(bx_v[...], recv3[...].astype(F32).reshape(256, C).astype(BF16))
    send4[...] = out4.astype(BF16).reshape(16, 4, 16, C)

    @pl.loop(0, 16)
    def _(s):
        copy_to(send4.at[s], modes_hbm.at[my_block], 5, (dp, s))

    arrived(modes_hbm, 5)
    out.wait()

    def sent(buf, stage):
        pltpu.make_async_copy(buf, buf, send_sem.at[stage]).wait()

    for k in range(2):
        sent(send1.at[k, pl.ds(0, 15)], k)
    sent(send4.at[pl.ds(0, 15)], 5)

    @pl.when(self_in)
    def _():
        for k in range(2):
            sent(send2.at[k, pl.ds(0, 31)], 2 + k)
        sent(send3.at[pl.ds(0, 31)], 4)

    @pl.when(jnp.logical_not(self_in))
    def _():
        for k in range(2):
            sent(send2.at[k], 2 + k)
        sent(send3, 4)


def exchange(field, cot, weights, yz, fx, bx):
    any_spec = pl.BlockSpec(memory_space=pl.ANY)
    return pl.pallas_call(
        kernel,
        out_shape=(
            jax.ShapeDtypeStruct((16, 4, 16, C), BF16),
            jax.ShapeDtypeStruct((8, C, C), F32),
        ),
        in_specs=[any_spec] * 6,
        out_specs=(any_spec, any_spec),
        scratch_shapes=[
            pltpu.VMEM((4, 512, C), BF16),
            pltpu.VMEM((4, 512, C), BF16),
            pltpu.VMEM((8, C, C), F32),
            pltpu.VMEM((256, 512), BF16),
            pltpu.VMEM((256, 1024), BF16),
            pltpu.VMEM((1024, 256), BF16),
            pltpu.VMEM((8, C, C), BF16),
            pltpu.VMEM((2, 16, 4, 16, C), BF16),
            pltpu.VMEM((2, 16, 4, 16, C), BF16),
            pltpu.VMEM((2, 32, 8, C), BF16),
            pltpu.VMEM((2, 32, 8, C), BF16),
            pltpu.VMEM((256, 1024), BF16),
            pltpu.VMEM((32, 8, C), BF16),
            pltpu.VMEM((16, 2, 8, C), BF16),
            pltpu.VMEM((16, 4, 16, C), BF16),
            pltpu.VMEM((8, C, C), F32),
            pltpu.SemaphoreType.DMA((6,)),
            pltpu.SemaphoreType.DMA,
            pltpu.SemaphoreType.DMA((6,)),
            pltpu.SemaphoreType.DMA((6,)),
        ],
        compiler_params=pltpu.CompilerParams(collective_id=0, has_side_effects=True),
    )(field, cot, weights, yz, fx, bx)


def adam_update(weights, first_moment, second_moment, weight_grads):
    new_first = decay_first * first_moment + (1.0 - decay_first) * weight_grads
    new_second = decay_second * second_moment + (1.0 - decay_second) * weight_grads * weight_grads
    first_hat = new_first / (1.0 - decay_first**STEP)
    second_hat = new_second / (1.0 - decay_second**STEP)
    new_weights = weights - learn_rate * first_hat / (jnp.sqrt(second_hat) + adam_floor)
    return (new_weights, new_first, new_second)


def on_device(field, cotangent, weights, first_moment, second_moment):
    yz, fx, bx, zy = (jnp.asarray(t) for t in tables())
    modes, grads = exchange(
        field.reshape(4, 512, C),
        cotangent.reshape(4, 512, C),
        weights.reshape(8, C, C),
        yz,
        fx,
        bx,
    )
    field_grad = jnp.einsum(
        "nk,xkc->xnc",
        zy,
        modes.transpose(1, 0, 2, 3).reshape(4, 256, C),
        preferred_element_type=F32,
    ).astype(BF16)
    new_weights, new_first, new_second = adam_update(
        weights, first_moment, second_moment, grads.reshape(weights.shape)
    )
    return (field_grad.reshape(field.shape), new_weights, new_first, new_second)


def solution(mesh):
    placed = (
        P("dp", "space", None, None, None),
        P("dp", "space", None, None, None),
        P("space", "dp", None, None, None),
        P("space", "dp", None, None, None),
        P("space", "dp", None, None, None),
    )
    return jax.shard_map(
        on_device,
        mesh=mesh,
        in_specs=placed,
        out_specs=(
            P("dp", "space", None, None, None),
            P("space", "dp", None, None, None),
            P("space", "dp", None, None, None),
            P("space", "dp", None, None, None),
        ),
        check_vma=False,
    )
```

time: 152 us -> 62.5 us (0.41)
  the two profiles are of different devices: /device:TPU:1 before, /device:TPU:8 now
where the time goes in v1:
time: 62.5 us; the launch traced here: 62.3 us
  Pallas kernels  56.9 us (91%)
  other arithmetic  2.42 us (4%)
  local copies, waits for them, and re-layouts  1.96 us (3%)
  between operations  0.71 us (1%)
    pallas_call x1, Pallas kernels, exchange(): pl.pallas_call(kernel, out_shape=(jax.ShapeDtypeStruct((16, 4, 16, C), BF...  56.9 us
    sub x1, other arithmetic, adam_update(): weights - learn_rate * first_hat / (jnp.sqrt(second_hat) + adam_floor)  2.42 us

profile of v1, /device:TPU:8, one launch (start us, length us, event | category | flops | bytes accessed | tf_op | source)
XLA Modules:
  0.0 62.3 jit_solution(1544285778432050051)
XLA Ops:
  0.6 0.0 copy-start
  0.6 0.0 copy-start.1
  0.7 0.0 copy-start.2
  0.7 56.9 %shard_map.120 = (bf16[16,4,16,128]{3,2,1,0:T(8,128)(2,1)}, f32[8,128,128]{2,1,0:T(8,128)}) custom-call(bf16[4,512,128]{2,1,0:T(8,128)(2,1)} %bitcast.16, bf16[4,512,128]{2,1,0:T(8,128)(2,1)} %bitcast.17, f32[8,128,128]{2,1,0:T(8,128)} %bitcast.12, bf16[256,512]{1,0:T(8,128)(2,1)} %constant.25.clone.yz_hbm, bf16[256,1024]{1,0:T(8,128)(2,1)} %constant.26.clone.fx_hbm, ...), custom_call_target="tpu_custom_call" | custom-call | tf_op jit(solution)/shard_map/pallas_call | solution.py:291
  57.5 0.0 copy-done
  57.5 0.0 copy-done.1
  57.6 0.0 copy-done.2
  57.6 0.0 copy-start.3
  57.6 2.4 %divide_subtract_fusion = (f32[1,4,2,128,128]{4,3,2,1,0:T(8,128)}, f32[1,4,2,128,128]{4,3,2,1,0:T(8,128)}, f32[1,4,2,128,128]{4,3,2,1,0:T(8,128)}) fusion(f32[1,4,2,128,128]{4,3,2,1,0:T(8,128)S(1)} %copy-done, f32[1,4,2,128,128]{4,3,2,1,0:T(8,128)} %bitcast.14, f32[1,4,2,128,128]{4,3,2,1,0:T(8,128)S(1)} %copy-done.1, f32[1,4,2,128,128]{4,3,2,1,0:T(8,128)S(1)} %copy-done.2), kind=kLoop, calls=%fused_computation.4 | loop fusion | flops 1572864 | bytes 3670016 | tf_op jit(solution)/shard_map/sub | solution.py:330
  60.0 0.0 copy-done.3
  60.0 0.0 copy-start.4
  60.0 0.9 %copy-done.4 = bf16[512,256,1]{1,0,2:T(8,128)(2,1)S(1)} copy-done((bf16[512,256,1]{1,0,2:T(8,128)(2,1)S(1)}, bf16[512,256,1]{1,0,2:T(8,128)(2,1)}, u32[]{:S(2)}) %copy-start.4) | copy-done | bytes 262168
  60.9 0.3 fusion
  61.3 1.0 %copy.16 = bf16[4,512,128]{2,1,0:T(8,128)(2,1)} copy(bf16[4,512,128]{1,2,0:T(8,128)(2,1)S(1)} %fusion) | data formatting | bytes 1048576 | tf_op jit(solution)/shard_map/convert_element_type | solution.py:349
  (1 shorter events, 0.0 us)
Async XLA Ops:
  0.6 56.9 %copy-start = (f32[1,4,2,128,128]{4,3,2,1,0:T(8,128)S(1)}, f32[1,4,2,128,128]{4,3,2,1,0:T(8,128)}, u32[]{:S(2)}) copy-start(f32[1,4,2,128,128]{4,3,2,1,0:T(8,128)} %param.11) | copy-start | bytes 1572868
  0.6 56.9 %copy-start.1 = (f32[1,4,2,128,128]{4,3,2,1,0:T(8,128)S(1)}, f32[1,4,2,128,128]{4,3,2,1,0:T(8,128)}, u32[]{:S(2)}) copy-start(f32[1,4,2,128,128]{4,3,2,1,0:T(8,128)} %param.12) | copy-start | bytes 1572868
  0.7 56.9 %copy-start.2 = (f32[1,4,2,128,128]{4,3,2,1,0:T(8,128)S(1)}, f32[1,4,2,128,128]{4,3,2,1,0:T(8,128)}, u32[]{:S(2)}) copy-start(f32[1,4,2,128,128]{4,3,2,1,0:T(8,128)} %param.13) | copy-start | bytes 1572868
  57.6 2.4 %copy-start.3 = (bf16[16,4,16,128]{3,2,1,0:T(8,128)(2,1)S(1)}, bf16[16,4,16,128]{3,2,1,0:T(8,128)(2,1)}, u32[]{:S(2)}) copy-start(bf16[16,4,16,128]{3,2,1,0:T(8,128)(2,1)} %get-tuple-element.6) | copy-start | bytes 786436
  60.0 1.0 %copy-start.4 = (bf16[512,256,1]{1,0,2:T(8,128)(2,1)S(1)}, bf16[512,256,1]{1,0,2:T(8,128)(2,1)}, u32[]{:S(2)}) copy-start(bf16[512,256,1]{1,0,2:T(8,128)(2,1)} %constant.34) | copy-start | bytes 786436

commit v2 on v1

v2 whole, which is shorter than its diff:
```python
import functools

import jax
import jax.numpy as jnp
import numpy as np
from jax import lax
from jax.experimental import pallas as pl
from jax.experimental.pallas import tpu as pltpu
from jax.sharding import PartitionSpec as P
import ml_dtypes

C = 128
MX = 16
MY = 16
MZ = 8
NX = 64
NY = 32
NZ = 16
STEP = 100
MYZ = 128

decay_first = 0.9
decay_second = 0.999
learn_rate = 0.001
adam_floor = 1e-08

VMEM_GRANT = 64 * 2**20 - 2240 * 1024

MESH = pl.DeviceIdType.MESH
BF16 = jnp.bfloat16
F32 = jnp.float32


def trig_tables(length, modes_kept, signed):
    points = np.arange(length)
    frequency = np.arange(modes_kept) - (modes_kept // 2 if signed else 0)
    phases = np.mod(points[:, None] * frequency[None, :], length).astype(np.float32)
    angles = (phases * np.float32(2.0 * np.pi / length)).astype(np.float32)
    factor = np.float32(1.0 / np.sqrt(length))
    cos_t = (np.cos(angles) * factor).astype(ml_dtypes.bfloat16).astype(np.float32)
    sin_t = (np.sin(angles) * factor).astype(ml_dtypes.bfloat16).astype(np.float32)
    return cos_t, sin_t


def complex_rows(re, im):
    return np.stack([np.stack([re, -im], axis=-1), np.stack([im, re], axis=-1)], axis=1)


@functools.cache
def tables():
    cos_z, sin_z = trig_tables(NZ, MZ, False)
    cos_y, sin_y = trig_tables(NY, MY, True)
    cos_x, sin_x = trig_tables(NX, MX, True)
    ez = cos_z - 1j * sin_z
    ey = cos_y - 1j * sin_y
    ex = cos_x - 1j * sin_x
    yz = np.einsum("ym,zk->mkyz", ey, ez)
    yz = np.stack([yz.real, yz.imag], axis=2).reshape(MYZ * 2, NY * NZ)
    zy = np.einsum("ym,zk->yzmk", ey.conj(), ez.conj())
    zy = np.stack([zy.real, -zy.imag], axis=4).reshape(NY * NZ, MYZ * 2)
    eye = np.eye(8)
    fx = complex_rows(ex.T.real, ex.T.imag)
    fx = np.einsum("msxr,pq->mpsxqr", fx, eye).reshape(MX * 16, NX * 16)
    bx = complex_rows(ex.conj().real, ex.conj().imag)
    bx = np.einsum("xsmr,pq->xpsmqr", bx, eye).reshape(NX * 16, MX * 16)
    return tuple(t.astype(ml_dtypes.bfloat16) for t in (yz, fx, bx, zy))


def tri(v):
    return lax.rem(v * (v + 1) // 2, 4)


def dot(a, b):
    return jnp.dot(a, b, preferred_element_type=F32)


def kernel(
    field_hbm,
    cot_hbm,
    w_hbm,
    first_hbm,
    second_hbm,
    yz_hbm,
    fx_hbm,
    bx_hbm,
    modes,
    new_w,
    new_first,
    new_second,
    cot_v,
    field_v,
    w_v,
    first_v,
    second_v,
    yz_v,
    fx_v,
    bx_v,
    half_v,
    send1,
    recv1,
    send2,
    recv2,
    big_g,
    send3,
    recv3,
    send4,
    in_sem,
    send_sem,
    recv_sem,
):
    dp = lax.axis_index("dp")
    sp = lax.axis_index("space")
    gx, gz, core = dp // 8, (dp // 2) % 4, dp % 2
    sy, sz = sp // 4, sp % 4
    mine = dp // 2
    mx, mz = mine // 4, mine % 4

    half_way = (sz + 2) % 4
    peer_z = (3 - sz, half_way, 3 - half_way, sz)
    peer_y = tuple((sy + i) % 4 for i in range(4))
    block_y = tuple(((gx + y + 2 * core) % 4) * 4 for y in peer_y)
    block_z = tuple((gz + 3 + (1 + 2 * core) * tri(z)) % 4 for z in peer_z)
    peers = [
        (peer_y[iy] * 4 + peer_z[iz], block_y[iy] + block_z[iz])
        for iz in range(4)
        for iy in (2, 1, 3, 0)
    ]
    my_block = peers[-1][1]
    self_in = my_block == mine

    holders = []
    for i in range(16):
        k = (sp + i) % 16
        for ic in range(2):
            c = (core + ic) % 2
            holders.append((2 * my_block + c, k, 2 * k + c))

    at_y, at_z, sample = {}, {}, {}
    for ic in range(2):
        c = (core + ic) % 2
        for i in range(4):
            x, z = (gx + i) % 4, (gz + i) % 4
            at_y[i, ic] = ((mx - x - 2 * c + 8) % 4) * 4
            at_z[i, ic] = tri(((1 + 2 * c) * (mz - z + 5)) % 4)
            sample["x", i] = x * 8
            sample["z", i] = z * 2
        sample["c", ic] = c
    samples = []
    for iz in (0, 2, 1, 3):
        for ix in (0, 2, 1, 3):
            for ic in range(2):
                b = sample["x", ix] + sample["z", iz] + sample["c", ic]
                samples.append((b, at_y[ix, ic] + at_z[iz, ic]))

    def load(k, src, dst):
        copy = pltpu.make_async_copy(src, dst, in_sem.at[k])
        copy.start()
        return copy

    loads = [load(0, yz_hbm, yz_v), load(1, cot_hbm, cot_v)]

    barrier = pltpu.get_barrier_semaphore()

    def hello(b, s):
        pl.semaphore_signal(barrier, inc=1, device_id=(b, s), device_id_type=MESH)

    for s, _ in peers[:-1]:
        hello(dp, s)
    for b, s in samples[1:]:
        hello(b, s)
    for b, s, _ in holders[1:]:
        hello(b, s)

    @pl.when(jnp.logical_not(self_in))
    def _():
        hello(*samples[0])
        hello(*holders[0][:2])

    loads += [
        load(2, field_hbm, field_v),
        load(3, fx_hbm, fx_v),
        load(4, w_hbm, w_v),
        load(5, bx_hbm, bx_v),
        load(6, first_hbm, first_v),
        load(7, second_hbm, second_v),
    ]

    def remote(src, dst, stage, b, s):
        pltpu.make_async_remote_copy(
            src_ref=src,
            dst_ref=dst,
            send_sem=send_sem.at[stage],
            recv_sem=recv_sem.at[stage],
            device_id=(b, s),
            device_id_type=MESH,
        ).start()

    def local(src, dst, stage):
        pltpu.make_async_copy(src, dst, recv_sem.at[stage]).start()

    def maybe_local(src, dst, stage, b, s):
        @pl.when(self_in)
        def _():
            local(src, dst, stage)

        @pl.when(jnp.logical_not(self_in))
        def _():
            remote(src, dst, stage, b, s)

    def arrived(buf, stage):
        with jax.named_scope(f"wait_recv{stage}"):
            pltpu.make_async_copy(buf, buf, recv_sem.at[stage]).wait()

    def yz_modes(k, slab):
        for x in range(4):
            out = dot(yz_v[...], slab[x])
            send1[k, :, x] = out.astype(BF16).reshape(16, 16, C)

    def send_slab(k):
        for s, q in peers[:-1]:
            remote(send1.at[k, q], recv1.at[k, sp], k, dp, s)
        local(send1.at[k, my_block], recv1.at[k, sp], k)

    def x_modes(k):
        out = dot(fx_v[...], recv1[k].reshape(1024, C))
        send2[k] = out.astype(BF16).reshape(32, 8, C)
        for b, s, m in holders[1:]:
            remote(send2.at[k, m], recv2.at[k, dp], 2 + k, b, s)
        b, s, m = holders[0]
        maybe_local(send2.at[k, m], recv2.at[k, dp], 2 + k, b, s)

    loads[0].wait()
    loads[1].wait()
    yz_modes(0, cot_v)

    with jax.named_scope("wait_barrier"):

        @pl.when(self_in)
        def _():
            pl.semaphore_wait(barrier, 15 + 62)

        @pl.when(jnp.logical_not(self_in))
        def _():
            pl.semaphore_wait(barrier, 15 + 64)

    send_slab(0)
    loads[2].wait()
    yz_modes(1, field_v)
    loads[3].wait()
    loads[4].wait()
    half_v[...] = w_v[...].astype(BF16)

    arrived(recv1.at[0], 0)
    x_modes(0)
    send_slab(1)

    arrived(recv2.at[0], 2)
    cot = recv2[0].astype(F32).reshape(256, C)
    row = lax.broadcasted_iota(jnp.int32, (256, C), 0)
    turned = jnp.where(
        lax.rem(row, 2) == 0, pltpu.roll(cot, 255, 0), -pltpu.roll(cot, 1, 0)
    )
    pencil = lax.rem(row // 2, 4)
    back = jnp.zeros((256, C), F32)
    for j in range(4):
        for part, rows in ((0, cot), (1, turned)):
            g = jnp.where(pencil == j, rows, 0.0).astype(BF16)
            big_g[:, pl.ds((2 * j + part) * C, C)] = g
            back += lax.dot_general(
                g, half_v[2 * j + part], (((1,), (1,)), ((), ())), preferred_element_type=F32
            )
    send3[...] = back.astype(BF16).reshape(32, 8, C)
    for b, s in samples[1:]:
        remote(send3.at[b], recv3.at[sp, core], 4, b, s)
    maybe_local(send3.at[dp], recv3.at[sp, core], 4, *samples[0])

    arrived(recv1.at[1], 1)
    x_modes(1)

    loads[5].wait()
    arrived(recv3, 4)
    out4 = dot(bx_v[...], recv3[...].astype(F32).reshape(256, C).astype(BF16))
    send4[...] = out4.astype(BF16).reshape(16, 4, 16, C)
    for s, _ in peers[:-1]:
        remote(send4.at[s], modes.at[my_block], 5, dp, s)
    local(send4.at[sp], modes.at[my_block], 5)

    loads[6].wait()
    loads[7].wait()
    arrived(recv2.at[1], 3)
    left = recv2[1].astype(F32).reshape(256, C).T.astype(BF16)
    for n in range(8):
        grads = dot(left, big_g[:, pl.ds(n * C, C)])
        new_w[n], new_first[n], new_second[n] = adam_update(
            w_v[n], first_v[n], second_v[n], grads
        )

    def sent(buf, stage):
        pltpu.make_async_copy(buf, buf, send_sem.at[stage]).wait()

    for k in range(2):
        sent(send1.at[k, pl.ds(0, 15)], k)

    @pl.when(self_in)
    def _():
        for k in range(2):
            sent(send2.at[k, pl.ds(0, 31)], 2 + k)
        sent(send3.at[pl.ds(0, 31)], 4)

    @pl.when(jnp.logical_not(self_in))
    def _():
        for k in range(2):
            sent(send2.at[k], 2 + k)
        sent(send3, 4)

    sent(send4.at[pl.ds(0, 15)], 5)
    arrived(modes, 5)


def exchange(field, cot, weights, first, second, yz, fx, bx):
    any_spec = pl.BlockSpec(memory_space=pl.ANY)
    vmem_spec = pl.BlockSpec(memory_space=pltpu.VMEM)
    part = pltpu.VMEM((8, C, C), F32)
    return pl.pallas_call(
        kernel,
        out_shape=(pltpu.VMEM((16, 4, 16, C), BF16), part, part, part),
        in_specs=[any_spec] * 8,
        out_specs=(vmem_spec,) * 4,
        scratch_shapes=[
            pltpu.VMEM((4, 512, C), BF16),
            pltpu.VMEM((4, 512, C), BF16),
            part,
            part,
            part,
            pltpu.VMEM((256, 512), BF16),
            pltpu.VMEM((256, 1024), BF16),
            pltpu.VMEM((1024, 256), BF16),
            pltpu.VMEM((8, C, C), BF16),
            pltpu.VMEM((2, 16, 4, 16, C), BF16),
            pltpu.VMEM((2, 16, 4, 16, C), BF16),
            pltpu.VMEM((2, 32, 8, C), BF16),
            pltpu.VMEM((2, 32, 8, C), BF16),
            pltpu.VMEM((256, 1024), BF16),
            pltpu.VMEM((32, 8, C), BF16),
            pltpu.VMEM((16, 2, 8, C), BF16),
            pltpu.VMEM((16, 4, 16, C), BF16),
            pltpu.SemaphoreType.DMA((8,)),
            pltpu.SemaphoreType.DMA((6,)),
            pltpu.SemaphoreType.DMA((6,)),
        ],
        compiler_params=pltpu.CompilerParams(
            collective_id=0, has_side_effects=True, vmem_limit_bytes=VMEM_GRANT
        ),
    )(field, cot, weights, first, second, yz, fx, bx)


def finish_kernel(
    modes, zy, new_w, new_first, new_second, grad_hbm, w_hbm, first_hbm, second_hbm, grad_v, sem
):
    copies = []

    def store(k, src, dst):
        copy = pltpu.make_async_copy(src, dst, sem.at[k])
        copy.start()
        copies.append(copy)

    store(0, new_w, w_hbm)
    store(1, new_first, first_hbm)
    store(2, new_second, second_hbm)
    for x in range(4):
        out = dot(zy[...], modes[:, x].reshape(256, C))
        grad_v[x] = out.astype(BF16)
        store(3 + x, grad_v.at[x], grad_hbm.at[x])
    for copy in copies:
        copy.wait()


def finish(modes, zy, new_w, new_first, new_second):
    any_spec = pl.BlockSpec(memory_space=pl.ANY)
    vmem_spec = pl.BlockSpec(memory_space=pltpu.VMEM)
    part = jax.ShapeDtypeStruct((8, C, C), F32)
    return pl.pallas_call(
        finish_kernel,
        out_shape=(jax.ShapeDtypeStruct((4, 512, C), BF16), part, part, part),
        in_specs=[vmem_spec] * 5,
        out_specs=(any_spec,) * 4,
        scratch_shapes=[pltpu.VMEM((4, 512, C), BF16), pltpu.SemaphoreType.DMA((7,))],
        compiler_params=pltpu.CompilerParams(vmem_limit_bytes=16 * 2**20),
    )(modes, zy, new_w, new_first, new_second)


def adam_update(weights, first_moment, second_moment, weight_grads):
    new_first = decay_first * first_moment + (1.0 - decay_first) * weight_grads
    new_second = decay_second * second_moment + (1.0 - decay_second) * weight_grads * weight_grads
    first_hat = new_first / (1.0 - decay_first**STEP)
    second_hat = new_second / (1.0 - decay_second**STEP)
    new_weights = weights - learn_rate * first_hat / (jnp.sqrt(second_hat) + adam_floor)
    return (new_weights, new_first, new_second)


def on_device(field, cotangent, weights, first_moment, second_moment):
    yz, fx, bx, zy = (jnp.asarray(t) for t in tables())
    modes, new_weights, new_first, new_second = exchange(
        field.reshape(4, 512, C),
        cotangent.reshape(4, 512, C),
        weights.reshape(8, C, C),
        first_moment.reshape(8, C, C),
        second_moment.reshape(8, C, C),
        yz,
        fx,
        bx,
    )
    field_grad, *state = finish(modes, zy, new_weights, new_first, new_second)
    return (field_grad.reshape(field.shape), *(a.reshape(weights.shape) for a in state))


def solution(mesh):
    placed = (
        P("dp", "space", None, None, None),
        P("dp", "space", None, None, None),
        P("space", "dp", None, None, None),
        P("space", "dp", None, None, None),
        P("space", "dp", None, None, None),
    )
    return jax.shard_map(
        on_device,
        mesh=mesh,
        in_specs=placed,
        out_specs=(
            P("dp", "space", None, None, None),
            P("space", "dp", None, None, None),
            P("space", "dp", None, None, None),
            P("space", "dp", None, None, None),
        ),
        check_vma=False,
    )
```

time: 62.5 us -> 56 us (0.90)
  other arithmetic: 2.42 us -> 0 us
  local copies, waits for them, and re-layouts: 1.96 us -> 0.01 us
  Pallas kernels: 56.9 us -> 55.2 us
    sub x1 -> x0, other arithmetic: 2.42 us -> none  [adam_update(): weights - learn_rate * first_hat / (jnp.sqrt(second_hat) + adam_floor)]
    pallas_call x1 -> x2, Pallas kernels: 56.9 us -> 55.2 us  [the longest x1 53.8 us: exchange(): pl.pallas_call(kernel, out_shape=(pltpu.VMEM((16, 4, 16, C), BF16), part,...]
    convert_element_type x1 -> x0, local copies, waits for them, and re-layouts: 1 us -> none  [on_device(): field_grad = jnp.einsum('nk,xkc->xnc', zy, modes.transpose(1, 0, 2, 3).re...]
    unnamed x10 -> x2, local copies, waits for them, and re-layouts: 0.95 us -> 0.01 us
where the time goes in v2:
time: 56 us; the launch traced here: 55.8 us
  Pallas kernels  55.2 us (99%)
  between operations  0.66 us (1%)
    pallas_call x1, Pallas kernels, exchange(): pl.pallas_call(kernel, out_shape=(pltpu.VMEM((16, 4, 16, C), BF16), part,...  53.8 us
    pallas_call x1, Pallas kernels, finish(): pl.pallas_call(finish_kernel, out_shape=(jax.ShapeDtypeStruct((4, 512, C)...  1.37 us

profile of v2, /device:TPU:8, one launch (start us, length us, event | category | flops | bytes accessed | tf_op | source)
XLA Modules:
  0.0 55.8 jit_solution(11142920221977319501)
XLA Ops:
  0.6 0.0 copy-start
  0.6 53.8 %shard_map.120 = (bf16[16,4,16,128]{3,2,1,0:T(8,128)(2,1)S(1)}, f32[8,128,128]{2,1,0:T(8,128)S(1)}, f32[8,128,128]{2,1,0:T(8,128)S(1)}, f32[8,128,128]{2,1,0:T(8,128)S(1)}) custom-call(bf16[4,512,128]{2,1,0:T(8,128)(2,1)} %bitcast.9, bf16[4,512,128]{2,1,0:T(8,128)(2,1)} %bitcast.10, f32[8,128,128]{2,1,0:T(8,128)} %bitcast.11, f32[8,128,128]{2,1,0:T(8,128)} %bitcast.12, ...), custom_call_target="tpu_custom_call" | custom-call | tf_op jit(solution)/shard_map/pallas_call | solution.py:324
  54.5 0.0 copy-done
  54.5 1.4 %shard_map.121 = (bf16[4,512,128]{2,1,0:T(8,128)(2,1)}, f32[8,128,128]{2,1,0:T(8,128)}, f32[8,128,128]{2,1,0:T(8,128)}, f32[8,128,128]{2,1,0:T(8,128)}) custom-call(bf16[16,4,16,128]{3,2,1,0:T(8,128)(2,1)S(1)} %get-tuple-element.12.modes, bf16[512,256]{1,0:T(8,128)(2,1)S(1)} %copy-done, f32[8,128,128]{2,1,0:T(8,128)S(1)} %get-tuple-element.13.new_w, ...), custom_call_target="tpu_custom_call" | custom-call | tf_op jit(solution)/shard_map/pallas_call | solution.py:382
Async XLA Ops:
  0.6 53.8 %copy-start = (bf16[512,256]{1,0:T(8,128)(2,1)S(1)}, bf16[512,256]{1,0:T(8,128)(2,1)}, u32[]{:S(2)}) copy-start(bf16[512,256]{1,0:T(8,128)(2,1)} %constant.11.clone.zy) | copy-start | bytes 786436

commit v3 on v2

--- a/solution.py
+++ b/solution.py
@@ -107,6 +107,7 @@
     in_sem,
     send_sem,
     recv_sem,
+    met,
 ):
     dp = lax.axis_index("dp")
     sp = lax.axis_index("space")
@@ -161,20 +162,20 @@
 
     barrier = pltpu.get_barrier_semaphore()
 
-    def hello(b, s):
-        pl.semaphore_signal(barrier, inc=1, device_id=(b, s), device_id_type=MESH)
-
+    def hello(sem, b, s):
+        pl.semaphore_signal(sem, inc=1, device_id=(b, s), device_id_type=MESH)
+
+    plane = [
+        (sample["x", ix] + gz * 2 + sample["c", ic], sp)
+        for ix in range(4)
+        for ic in range(2)
+        if ix or ic
+    ]
+    beside = [(gx * 8 + sample["z", iz] + core, sp) for iz in (1, 3)]
     for s, _ in peers[:-1]:
-        hello(dp, s)
-    for b, s in samples[1:]:
-        hello(b, s)
-    for b, s, _ in holders[1:]:
-        hello(b, s)
-
-    @pl.when(jnp.logical_not(self_in))
-    def _():
-        hello(*samples[0])
-        hello(*holders[0][:2])
+        hello(barrier, dp, s)
+    for b, s in plane + beside:
+        hello(barrier, b, s)
 
     loads += [
         load(2, field_hbm, field_v),
@@ -224,6 +225,8 @@
     def x_modes(k):
         out = dot(fx_v[...], recv1[k].reshape(1024, C))
         send2[k] = out.astype(BF16).reshape(32, 8, C)
+        if k == 0:
+            pl.semaphore_wait(met.at[2], 2)
         for b, s, m in holders[1:]:
             remote(send2.at[k, m], recv2.at[k, dp], 2 + k, b, s)
         b, s, m = holders[0]
@@ -234,21 +237,22 @@
     yz_modes(0, cot_v)
 
     with jax.named_scope("wait_barrier"):
-
-        @pl.when(self_in)
-        def _():
-            pl.semaphore_wait(barrier, 15 + 62)
-
-        @pl.when(jnp.logical_not(self_in))
-        def _():
-            pl.semaphore_wait(barrier, 15 + 64)
+        pl.semaphore_wait(barrier, 15 + 7 + 2)
 
     send_slab(0)
+    for b, s in plane:
+        hello(met.at[0], b, s)
     loads[2].wait()
     yz_modes(1, field_v)
+    pl.semaphore_wait(met.at[0], 7)
+    for b, s in beside:
+        hello(met.at[1], b, s)
     loads[3].wait()
     loads[4].wait()
     half_v[...] = w_v[...].astype(BF16)
+    pl.semaphore_wait(met.at[1], 2)
+    for b, s in beside:
+        hello(met.at[2], b, s)
 
     arrived(recv1.at[0], 0)
     x_modes(0)
@@ -347,6 +351,7 @@
             pltpu.SemaphoreType.DMA((8,)),
             pltpu.SemaphoreType.DMA((6,)),
             pltpu.SemaphoreType.DMA((6,)),
+            pltpu.SemaphoreType.REGULAR((3,)),
         ],
         compiler_params=pltpu.CompilerParams(
             collective_id=0, has_side_effects=True, vmem_limit_bytes=VMEM_GRANT

time: 56 us -> 52.1 us (0.930)
  the two profiles are of different devices: /device:TPU:8 before, /device:TPU:2 now
where the time goes in v3:
time: 52.1 us; the launch traced here: 52 us
  Pallas kernels  51.3 us (98%)
  between operations  0.66 us (1%)
    pallas_call x1, Pallas kernels, exchange(): pl.pallas_call(kernel, out_shape=(pltpu.VMEM((16, 4, 16, C), BF16), part,...  50 us
    pallas_call x1, Pallas kernels, finish(): pl.pallas_call(finish_kernel, out_shape=(jax.ShapeDtypeStruct((4, 512, C)...  1.37 us

profile of v3, /device:TPU:2, one launch (start us, length us, event | category | flops | bytes accessed | tf_op | source)
XLA Modules:
  0.0 52.0 jit_solution(7361205748769960053)
XLA Ops:
  0.6 0.0 copy-start
  0.6 50.0 %shard_map.120 = (bf16[16,4,16,128]{3,2,1,0:T(8,128)(2,1)S(1)}, f32[8,128,128]{2,1,0:T(8,128)S(1)}, f32[8,128,128]{2,1,0:T(8,128)S(1)}, f32[8,128,128]{2,1,0:T(8,128)S(1)}) custom-call(bf16[4,512,128]{2,1,0:T(8,128)(2,1)} %bitcast.9, bf16[4,512,128]{2,1,0:T(8,128)(2,1)} %bitcast.10, f32[8,128,128]{2,1,0:T(8,128)} %bitcast.11, f32[8,128,128]{2,1,0:T(8,128)} %bitcast.12, ...), custom_call_target="tpu_custom_call" | custom-call | tf_op jit(solution)/shard_map/pallas_call | solution.py:328
  50.6 0.0 copy-done
  50.6 1.4 %shard_map.121 = (bf16[4,512,128]{2,1,0:T(8,128)(2,1)}, f32[8,128,128]{2,1,0:T(8,128)}, f32[8,128,128]{2,1,0:T(8,128)}, f32[8,128,128]{2,1,0:T(8,128)}) custom-call(bf16[16,4,16,128]{3,2,1,0:T(8,128)(2,1)S(1)} %get-tuple-element.12.modes, bf16[512,256]{1,0:T(8,128)(2,1)S(1)} %copy-done, f32[8,128,128]{2,1,0:T(8,128)S(1)} %get-tuple-element.13.new_w, ...), custom_call_target="tpu_custom_call" | custom-call | tf_op jit(solution)/shard_map/pallas_call | solution.py:387
Async XLA Ops:
  0.6 50.0 %copy-start = (bf16[512,256]{1,0:T(8,128)(2,1)S(1)}, bf16[512,256]{1,0:T(8,128)(2,1)}, u32[]{:S(2)}) copy-start(bf16[512,256]{1,0:T(8,128)(2,1)} %constant.11.clone.zy) | copy-start | bytes 786436

commit v4 on v3

--- a/solution.py
+++ b/solution.py
@@ -55,19 +55,21 @@
     ey = cos_y - 1j * sin_y
     ex = cos_x - 1j * sin_x
     yz = np.einsum("ym,zk->mkyz", ey, ez)
-    yz = np.stack([yz.real, yz.imag], axis=2).reshape(MYZ * 2, NY * NZ)
+    yz = np.stack([yz.real, yz.imag], axis=2).reshape(16, 2, 8, NY * NZ)
+    yz = yz.transpose(1, 0, 2, 3).reshape(MYZ * 2, NY * NZ)
     zy = np.einsum("ym,zk->yzmk", ey.conj(), ez.conj())
-    zy = np.stack([zy.real, -zy.imag], axis=4).reshape(NY * NZ, MYZ * 2)
-    eye = np.eye(8)
+    zy = np.stack([zy.real, -zy.imag], axis=4).reshape(NY * NZ, 16, 2, 8)
+    zy = zy.transpose(0, 2, 1, 3).reshape(NY * NZ, MYZ * 2)
+    eye = np.eye(4)
     fx = complex_rows(ex.T.real, ex.T.imag)
-    fx = np.einsum("msxr,pq->mpsxqr", fx, eye).reshape(MX * 16, NX * 16)
+    fx = np.einsum("msxr,pq->mpsxqr", fx, eye).reshape(MX * 8, NX * 8)
     bx = complex_rows(ex.conj().real, ex.conj().imag)
-    bx = np.einsum("xsmr,pq->xpsmqr", bx, eye).reshape(NX * 16, MX * 16)
+    bx = np.einsum("xsmr,pq->xpsmqr", bx, eye).reshape(NX * 8, MX * 8)
     return tuple(t.astype(ml_dtypes.bfloat16) for t in (yz, fx, bx, zy))
 
 
 def tri(v):
-    return lax.rem(v * (v + 1) // 2, 4)
+    return ((v * (v + 1)) >> 1) & 3
 
 
 def dot(a, b):
@@ -111,16 +113,58 @@
 ):
     dp = lax.axis_index("dp")
     sp = lax.axis_index("space")
-    gx, gz, core = dp // 8, (dp // 2) % 4, dp % 2
-    sy, sz = sp // 4, sp % 4
-    mine = dp // 2
-    mx, mz = mine // 4, mine % 4
-
-    half_way = (sz + 2) % 4
+
+    def load(k, src, dst):
+        copy = pltpu.make_async_copy(src, dst, in_sem.at[k])
+        copy.start()
+        return copy
+
+    loads = [load(0, yz_hbm, yz_v), load(1, cot_hbm, cot_v)]
+
+    def hello(sem, b, s):
+        pl.semaphore_signal(sem, inc=1, device_id=(b, s), device_id_type=MESH)
+
+    barrier = pltpu.get_barrier_semaphore()
+    level = dp & 6
+    plane = [level + 8 * x + c for x in range(4) for c in range(2)]
+    beside = [dp - level + ((dp + 2) & 6), dp - level + ((dp + 6) & 6)]
+
+    def hello_plane(sem):
+        for b in plane:
+
+            @pl.when(b != dp)
+            def _():
+                hello(sem, b, sp)
+
+    for k in range(16):
+
+        @pl.when(sp != k)
+        def _():
+            hello(barrier, dp, k)
+
+    hello_plane(barrier)
+    for b in beside:
+        hello(barrier, b, sp)
+
+    loads += [
+        load(2, field_hbm, field_v),
+        load(3, fx_hbm, fx_v),
+        load(4, w_hbm, w_v),
+        load(5, bx_hbm, bx_v),
+        load(6, first_hbm, first_v),
+        load(7, second_hbm, second_v),
+    ]
+
+    gx, gz, core = dp >> 3, (dp >> 1) & 3, dp & 1
+    sy, sz = sp >> 2, sp & 3
+    mine = dp >> 1
+    mx, mz = mine >> 2, mine & 3
+
+    half_way = (sz + 2) & 3
     peer_z = (3 - sz, half_way, 3 - half_way, sz)
-    peer_y = tuple((sy + i) % 4 for i in range(4))
-    block_y = tuple(((gx + y + 2 * core) % 4) * 4 for y in peer_y)
-    block_z = tuple((gz + 3 + (1 + 2 * core) * tri(z)) % 4 for z in peer_z)
+    peer_y = tuple((sy + i) & 3 for i in range(4))
+    block_y = tuple(((gx + y + 2 * core) & 3) * 4 for y in peer_y)
+    block_z = tuple((gz + 3 + (1 + 2 * core) * tri(z)) & 3 for z in peer_z)
     peers = [
         (peer_y[iy] * 4 + peer_z[iz], block_y[iy] + block_z[iz])
         for iz in range(4)
@@ -128,21 +172,15 @@
     ]
     my_block = peers[-1][1]
     self_in = my_block == mine
-
-    holders = []
-    for i in range(16):
-        k = (sp + i) % 16
-        for ic in range(2):
-            c = (core + ic) % 2
-            holders.append((2 * my_block + c, k, 2 * k + c))
+    far_block = ((block_z[3] - gz) & 3) == 2
 
     at_y, at_z, sample = {}, {}, {}
     for ic in range(2):
-        c = (core + ic) % 2
+        c = (core + ic) & 1
         for i in range(4):
-            x, z = (gx + i) % 4, (gz + i) % 4
-            at_y[i, ic] = ((mx - x - 2 * c + 8) % 4) * 4
-            at_z[i, ic] = tri(((1 + 2 * c) * (mz - z + 5)) % 4)
+            x, z = (gx + i) & 3, (gz + i) & 3
+            at_y[i, ic] = ((mx - x - 2 * c + 8) & 3) * 4
+            at_z[i, ic] = tri(((1 + 2 * c) * (mz - z + 5)) & 3)
             sample["x", i] = x * 8
             sample["z", i] = z * 2
         sample["c", ic] = c
@@ -153,60 +191,27 @@
                 b = sample["x", ix] + sample["z", iz] + sample["c", ic]
                 samples.append((b, at_y[ix, ic] + at_z[iz, ic]))
 
-    def load(k, src, dst):
-        copy = pltpu.make_async_copy(src, dst, in_sem.at[k])
-        copy.start()
-        return copy
-
-    loads = [load(0, yz_hbm, yz_v), load(1, cot_hbm, cot_v)]
-
-    barrier = pltpu.get_barrier_semaphore()
-
-    def hello(sem, b, s):
-        pl.semaphore_signal(sem, inc=1, device_id=(b, s), device_id_type=MESH)
-
-    plane = [
-        (sample["x", ix] + gz * 2 + sample["c", ic], sp)
-        for ix in range(4)
-        for ic in range(2)
-        if ix or ic
-    ]
-    beside = [(gx * 8 + sample["z", iz] + core, sp) for iz in (1, 3)]
-    for s, _ in peers[:-1]:
-        hello(barrier, dp, s)
-    for b, s in plane + beside:
-        hello(barrier, b, s)
-
-    loads += [
-        load(2, field_hbm, field_v),
-        load(3, fx_hbm, fx_v),
-        load(4, w_hbm, w_v),
-        load(5, bx_hbm, bx_v),
-        load(6, first_hbm, first_v),
-        load(7, second_hbm, second_v),
-    ]
-
-    def remote(src, dst, stage, b, s):
+    def remote(src, dst, send, recv, b, s):
         pltpu.make_async_remote_copy(
             src_ref=src,
             dst_ref=dst,
-            send_sem=send_sem.at[stage],
-            recv_sem=recv_sem.at[stage],
+            send_sem=send_sem.at[send],
+            recv_sem=recv_sem.at[recv],
             device_id=(b, s),
             device_id_type=MESH,
         ).start()
 
-    def local(src, dst, stage):
-        pltpu.make_async_copy(src, dst, recv_sem.at[stage]).start()
-
-    def maybe_local(src, dst, stage, b, s):
-        @pl.when(self_in)
+    def local(src, dst, recv):
+        pltpu.make_async_copy(src, dst, recv_sem.at[recv]).start()
+
+    def maybe_local(here, src, dst, send, recv, b, s):
+        @pl.when(here)
         def _():
-            local(src, dst, stage)
-
-        @pl.when(jnp.logical_not(self_in))
+            local(src, dst, recv)
+
+        @pl.when(jnp.logical_not(here))
         def _():
-            remote(src, dst, stage, b, s)
+            remote(src, dst, send, recv, b, s)
 
     def arrived(buf, stage):
         with jax.named_scope(f"wait_recv{stage}"):
@@ -215,22 +220,24 @@
     def yz_modes(k, slab):
         for x in range(4):
             out = dot(yz_v[...], slab[x])
-            send1[k, :, x] = out.astype(BF16).reshape(16, 16, C)
-
-    def send_slab(k):
+            send1[k, :, x] = out.astype(BF16).reshape(32, 8, C)
+
+    def send_slab(k, c, stage):
         for s, q in peers[:-1]:
-            remote(send1.at[k, q], recv1.at[k, sp], k, dp, s)
-        local(send1.at[k, my_block], recv1.at[k, sp], k)
-
-    def x_modes(k):
-        out = dot(fx_v[...], recv1[k].reshape(1024, C))
-        send2[k] = out.astype(BF16).reshape(32, 8, C)
-        if k == 0:
-            pl.semaphore_wait(met.at[2], 2)
-        for b, s, m in holders[1:]:
-            remote(send2.at[k, m], recv2.at[k, dp], 2 + k, b, s)
-        b, s, m = holders[0]
-        maybe_local(send2.at[k, m], recv2.at[k, dp], 2 + k, b, s)
+            remote(send1.at[k, 16 * c + q], recv1.at[k, 16 * c + sp], stage, stage, dp, s)
+        local(send1.at[k, 16 * c + my_block], recv1.at[k, 16 * c + sp], stage)
+
+    def x_modes(k, c):
+        slab = recv1[k, pl.ds(16 * c, 16)].reshape(512, C)
+        send2[k, pl.ds(16 * c, 16)] = dot(fx_v[...], slab).astype(BF16).reshape(16, 8, C)
+
+    def send_modes(k, c):
+        b = 2 * my_block + c
+        for i in range(1, 16):
+            s = (sp + i) & 15
+            remote(send2.at[k, 16 * c + s], recv2.at[k, dp], 3 + k, 3 + k, b, s)
+        here = jnp.logical_and(self_in, core == c)
+        maybe_local(here, send2.at[k, 16 * c + sp], recv2.at[k, dp], 3 + k, 3 + k, b, sp)
 
     loads[0].wait()
     loads[1].wait()
@@ -239,26 +246,40 @@
     with jax.named_scope("wait_barrier"):
         pl.semaphore_wait(barrier, 15 + 7 + 2)
 
-    send_slab(0)
-    for b, s in plane:
-        hello(met.at[0], b, s)
+    send_slab(0, 0, 0)
+    hello_plane(met.at[0])
+    send_slab(0, 1, 1)
     loads[2].wait()
     yz_modes(1, field_v)
     pl.semaphore_wait(met.at[0], 7)
-    for b, s in beside:
-        hello(met.at[1], b, s)
+    for b in beside:
+        hello(met.at[1], b, sp)
     loads[3].wait()
     loads[4].wait()
     half_v[...] = w_v[...].astype(BF16)
     pl.semaphore_wait(met.at[1], 2)
-    for b, s in beside:
-        hello(met.at[2], b, s)
-
-    arrived(recv1.at[0], 0)
-    x_modes(0)
-    send_slab(1)
-
-    arrived(recv2.at[0], 2)
+    for b in beside:
+        hello(met.at[2], b, sp)
+
+    arrived(recv1.at[0, pl.ds(0, 16)], 0)
+    x_modes(0, 0)
+
+    @pl.when(far_block)
+    def _():
+        pl.semaphore_wait(met.at[2], 2)
+
+    send_modes(0, 0)
+    arrived(recv1.at[0, pl.ds(16, 16)], 1)
+    x_modes(0, 1)
+    send_modes(0, 1)
+    send_slab(1, 0, 2)
+    send_slab(1, 1, 2)
+
+    @pl.when(jnp.logical_not(far_block))
+    def _():
+        pl.semaphore_wait(met.at[2], 2)
+
+    arrived(recv2.at[0], 3)
     cot = recv2[0].astype(F32).reshape(256, C)
     row = lax.broadcasted_iota(jnp.int32, (256, C), 0)
     turned = jnp.where(
@@ -275,23 +296,26 @@
             )
     send3[...] = back.astype(BF16).reshape(32, 8, C)
     for b, s in samples[1:]:
-        remote(send3.at[b], recv3.at[sp, core], 4, b, s)
-    maybe_local(send3.at[dp], recv3.at[sp, core], 4, *samples[0])
-
-    arrived(recv1.at[1], 1)
-    x_modes(1)
+        remote(send3.at[b], recv3.at[core, sp], 5, 5 + core, b, s)
+    maybe_local(self_in, send3.at[dp], recv3.at[core, sp], 5, 5 + core, *samples[0])
+
+    arrived(recv1.at[1], 2)
+    for c in range(2):
+        x_modes(1, c)
+        send_modes(1, c)
 
     loads[5].wait()
-    arrived(recv3, 4)
-    out4 = dot(bx_v[...], recv3[...].astype(F32).reshape(256, C).astype(BF16))
-    send4[...] = out4.astype(BF16).reshape(16, 4, 16, C)
-    for s, _ in peers[:-1]:
-        remote(send4.at[s], modes.at[my_block], 5, dp, s)
-    local(send4.at[sp], modes.at[my_block], 5)
+    for c in range(2):
+        arrived(recv3.at[c], 5 + c)
+        out4 = dot(bx_v[...], recv3[c].reshape(128, C))
+        send4[pl.ds(16 * c, 16)] = out4.astype(BF16).reshape(16, 4, 8, C)
+        for s, _ in peers[:-1]:
+            remote(send4.at[16 * c + s], modes.at[16 * c + my_block], 7 + c, 7 + c, dp, s)
+        local(send4.at[16 * c + sp], modes.at[16 * c + my_block], 7 + c)
 
     loads[6].wait()
     loads[7].wait()
-    arrived(recv2.at[1], 3)
+    arrived(recv2.at[1], 4)
     left = recv2[1].astype(F32).reshape(256, C).T.astype(BF16)
     for n in range(8):
         grads = dot(left, big_g[:, pl.ds(n * C, C)])
@@ -302,23 +326,25 @@
     def sent(buf, stage):
         pltpu.make_async_copy(buf, buf, send_sem.at[stage]).wait()
 
-    for k in range(2):
-        sent(send1.at[k, pl.ds(0, 15)], k)
+    for c in range(2):
+        sent(send1.at[0, pl.ds(0, 15)], c)
+        sent(send4.at[pl.ds(0, 15)], 7 + c)
+    sent(send1.at[1, pl.ds(0, 30)], 2)
 
     @pl.when(self_in)
     def _():
         for k in range(2):
-            sent(send2.at[k, pl.ds(0, 31)], 2 + k)
-        sent(send3.at[pl.ds(0, 31)], 4)
+            sent(send2.at[k, pl.ds(0, 31)], 3 + k)
+        sent(send3.at[pl.ds(0, 31)], 5)
 
     @pl.when(jnp.logical_not(self_in))
     def _():
         for k in range(2):
-            sent(send2.at[k], 2 + k)
-        sent(send3, 4)
-
-    sent(send4.at[pl.ds(0, 15)], 5)
-    arrived(modes, 5)
+            sent(send2.at[k], 3 + k)
+        sent(send3, 5)
+
+    for c in range(2):
+        arrived(modes.at[pl.ds(16 * c, 16)], 7 + c)
 
 
 def exchange(field, cot, weights, first, second, yz, fx, bx):
@@ -327,7 +353,7 @@
     part = pltpu.VMEM((8, C, C), F32)
     return pl.pallas_call(
         kernel,
-        out_shape=(pltpu.VMEM((16, 4, 16, C), BF16), part, part, part),
+        out_shape=(pltpu.VMEM((32, 4, 8, C), BF16), part, part, part),
         in_specs=[any_spec] * 8,
         out_specs=(vmem_spec,) * 4,
         scratch_shapes=[
@@ -337,20 +363,20 @@
             part,
             part,
             pltpu.VMEM((256, 512), BF16),
-            pltpu.VMEM((256, 1024), BF16),
-            pltpu.VMEM((1024, 256), BF16),
+            pltpu.VMEM((128, 512), BF16),
+            pltpu.VMEM((512, 128), BF16),
             pltpu.VMEM((8, C, C), BF16),
-            pltpu.VMEM((2, 16, 4, 16, C), BF16),
-            pltpu.VMEM((2, 16, 4, 16, C), BF16),
+            pltpu.VMEM((2, 32, 4, 8, C), BF16),
+            pltpu.VMEM((2, 32, 4, 8, C), BF16),
             pltpu.VMEM((2, 32, 8, C), BF16),
             pltpu.VMEM((2, 32, 8, C), BF16),
             pltpu.VMEM((256, 1024), BF16),
             pltpu.VMEM((32, 8, C), BF16),
-            pltpu.VMEM((16, 2, 8, C), BF16),
-            pltpu.VMEM((16, 4, 16, C), BF16),
+            pltpu.VMEM((2, 16, 8, C), BF16),
+            pltpu.VMEM((32, 4, 8, C), BF16),
             pltpu.SemaphoreType.DMA((8,)),
-            pltpu.SemaphoreType.DMA((6,)),
-            pltpu.SemaphoreType.DMA((6,)),
+            pltpu.SemaphoreType.DMA((9,)),
+            pltpu.SemaphoreType.DMA((9,)),
             pltpu.SemaphoreType.REGULAR((3,)),
         ],
         compiler_params=pltpu.CompilerParams(

time: 52.1 us -> 50.5 us (0.969)
  the two profiles are of different devices: /device:TPU:2 before, /device:TPU:1 now
where the time goes in v4:
time: 50.5 us; the launch traced here: 49.8 us
  Pallas kernels  49.1 us (97%)
  between operations  0.66 us (1%)
    pallas_call x1, Pallas kernels, exchange(): pl.pallas_call(kernel, out_shape=(pltpu.VMEM((32, 4, 8, C), BF16), part,...  47.7 us
    pallas_call x1, Pallas kernels, finish(): pl.pallas_call(finish_kernel, out_shape=(jax.ShapeDtypeStruct((4, 512, C)...  1.38 us

profile of v4, /device:TPU:1, one launch (start us, length us, event | category | flops | bytes accessed | tf_op | source)
XLA Modules:
  0.0 49.8 jit_solution(6473407250238700912)
XLA Ops:
  0.6 0.0 copy-start
  0.6 47.7 %shard_map.120 = (bf16[32,4,8,128]{3,2,1,0:T(8,128)(2,1)S(1)}, f32[8,128,128]{2,1,0:T(8,128)S(1)}, f32[8,128,128]{2,1,0:T(8,128)S(1)}, f32[8,128,128]{2,1,0:T(8,128)S(1)}) custom-call(bf16[4,512,128]{2,1,0:T(8,128)(2,1)} %bitcast.9, bf16[4,512,128]{2,1,0:T(8,128)(2,1)} %bitcast.10, f32[8,128,128]{2,1,0:T(8,128)} %bitcast.11, f32[8,128,128]{2,1,0:T(8,128)} %bitcast.12, ...), custom_call_target="tpu_custom_call" | custom-call | tf_op jit(solution)/shard_map/pallas_call | solution.py:354
  48.4 0.0 copy-done
  48.4 1.4 %shard_map.121 = (bf16[4,512,128]{2,1,0:T(8,128)(2,1)}, f32[8,128,128]{2,1,0:T(8,128)}, f32[8,128,128]{2,1,0:T(8,128)}, f32[8,128,128]{2,1,0:T(8,128)}) custom-call(bf16[32,4,8,128]{3,2,1,0:T(8,128)(2,1)S(1)} %get-tuple-element.12.modes, bf16[512,256]{1,0:T(8,128)(2,1)S(1)} %copy-done, f32[8,128,128]{2,1,0:T(8,128)S(1)} %get-tuple-element.13.new_w, ...), custom_call_target="tpu_custom_call" | custom-call | tf_op jit(solution)/shard_map/pallas_call | solution.py:413
Async XLA Ops:
  0.6 47.7 %copy-start = (bf16[512,256]{1,0:T(8,128)(2,1)S(1)}, bf16[512,256]{1,0:T(8,128)(2,1)}, u32[]{:S(2)}) copy-start(bf16[512,256]{1,0:T(8,128)(2,1)} %constant.11.clone.zy) | copy-start | bytes 786436

commit v5 on v4

--- a/solution.py
+++ b/solution.py
@@ -125,37 +125,17 @@
         pl.semaphore_signal(sem, inc=1, device_id=(b, s), device_id_type=MESH)
 
     barrier = pltpu.get_barrier_semaphore()
-    level = dp & 6
-    plane = [level + 8 * x + c for x in range(4) for c in range(2)]
-    beside = [dp - level + ((dp + 2) & 6), dp - level + ((dp + 6) & 6)]
-
-    def hello_plane(sem):
-        for b in plane:
-
-            @pl.when(b != dp)
-            def _():
-                hello(sem, b, sp)
-
+    core = dp & 1
+    first_core = core == 0
+    second_core = core == 1
+    chip = dp - core
     for k in range(16):
 
-        @pl.when(sp != k)
-        def _():
-            hello(barrier, dp, k)
-
-    hello_plane(barrier)
-    for b in beside:
-        hello(barrier, b, sp)
-
-    loads += [
-        load(2, field_hbm, field_v),
-        load(3, fx_hbm, fx_v),
-        load(4, w_hbm, w_v),
-        load(5, bx_hbm, bx_v),
-        load(6, first_hbm, first_v),
-        load(7, second_hbm, second_v),
-    ]
-
-    gx, gz, core = dp >> 3, (dp >> 1) & 3, dp & 1
+        @pl.when(jnp.logical_or(sp != k, second_core))
+        def _():
+            hello(barrier, chip, k)
+
+    gx, gz = dp >> 3, (dp >> 1) & 3
     sy, sz = sp >> 2, sp & 3
     mine = dp >> 1
     mx, mz = mine >> 2, mine & 3
@@ -172,7 +152,6 @@
     ]
     my_block = peers[-1][1]
     self_in = my_block == mine
-    far_block = ((block_z[3] - gz) & 3) == 2
 
     at_y, at_z, sample = {}, {}, {}
     for ic in range(2):
@@ -191,6 +170,16 @@
                 b = sample["x", ix] + sample["z", iz] + sample["c", ic]
                 samples.append((b, at_y[ix, ic] + at_z[iz, ic]))
 
+    for b, s in samples[2:]:
+        hello(barrier, b | 1, s)
+    for b, s in samples[:2]:
+
+        @pl.when(jnp.logical_or(first_core, s != sp))
+        def _():
+            hello(barrier, b | 1, s)
+
+    own_holder = jnp.logical_or(samples[0][1] == sp, samples[1][1] == sp)
+
     def remote(src, dst, send, recv, b, s):
         pltpu.make_async_remote_copy(
             src_ref=src,
@@ -241,32 +230,54 @@
 
     loads[0].wait()
     loads[1].wait()
+    loads += [
+        load(2, field_hbm, field_v),
+        load(3, fx_hbm, fx_v),
+        load(4, w_hbm, w_v),
+        load(5, bx_hbm, bx_v),
+        load(6, first_hbm, first_v),
+        load(7, second_hbm, second_v),
+    ]
     yz_modes(0, cot_v)
 
     with jax.named_scope("wait_barrier"):
-        pl.semaphore_wait(barrier, 15 + 7 + 2)
+
+        @pl.when(first_core)
+        def _():
+            pl.semaphore_wait(barrier, 31)
+            hello(met.at[0], dp + 1, sp)
+
+        @pl.when(second_core)
+        def _():
+            pl.semaphore_wait(met.at[0], 1)
 
     send_slab(0, 0, 0)
-    hello_plane(met.at[0])
     send_slab(0, 1, 1)
     loads[2].wait()
     yz_modes(1, field_v)
-    pl.semaphore_wait(met.at[0], 7)
-    for b in beside:
-        hello(met.at[1], b, sp)
     loads[3].wait()
     loads[4].wait()
     half_v[...] = w_v[...].astype(BF16)
-    pl.semaphore_wait(met.at[1], 2)
-    for b in beside:
-        hello(met.at[2], b, sp)
+
+    @pl.when(second_core)
+    def _():
+        @pl.when(own_holder)
+        def _():
+            pl.semaphore_wait(barrier, 63)
+
+        @pl.when(jnp.logical_not(own_holder))
+        def _():
+            pl.semaphore_wait(barrier, 64)
+
+        hello(met.at[1], chip, sp)
 
     arrived(recv1.at[0, pl.ds(0, 16)], 0)
     x_modes(0, 0)
 
-    @pl.when(far_block)
+    @pl.when(first_core)
     def _():
-        pl.semaphore_wait(met.at[2], 2)
+        with jax.named_scope("wait_far0"):
+            pl.semaphore_wait(met.at[1], 1)
 
     send_modes(0, 0)
     arrived(recv1.at[0, pl.ds(16, 16)], 1)
@@ -274,10 +285,6 @@
     send_modes(0, 1)
     send_slab(1, 0, 2)
     send_slab(1, 1, 2)
-
-    @pl.when(jnp.logical_not(far_block))
-    def _():
-        pl.semaphore_wait(met.at[2], 2)
 
     arrived(recv2.at[0], 3)
     cot = recv2[0].astype(F32).reshape(256, C)
@@ -377,7 +384,7 @@
             pltpu.SemaphoreType.DMA((8,)),
             pltpu.SemaphoreType.DMA((9,)),
             pltpu.SemaphoreType.DMA((9,)),
-            pltpu.SemaphoreType.REGULAR((3,)),
+            pltpu.SemaphoreType.REGULAR((2,)),
         ],
         compiler_params=pltpu.CompilerParams(
             collective_id=0, has_side_effects=True, vmem_limit_bytes=VMEM_GRANT

time: 50.5 us -> 47.3 us (0.937)
  Pallas kernels: 49.1 us -> 46.1 us
    pallas_call x1, Pallas kernels: 47.7 us -> 44.8 us  [exchange(): pl.pallas_call(kernel, out_shape=(pltpu.VMEM((32, 4, 8, C), BF16), part,...]
where the time goes in v5:
time: 47.3 us; the launch traced here: 46.8 us
  Pallas kernels  46.1 us (97%)
  between operations  0.66 us (1%)
    pallas_call x1, Pallas kernels, exchange(): pl.pallas_call(kernel, out_shape=(pltpu.VMEM((32, 4, 8, C), BF16), part,...  44.8 us
    pallas_call x1, Pallas kernels, finish(): pl.pallas_call(finish_kernel, out_shape=(jax.ShapeDtypeStruct((4, 512, C)...  1.38 us

profile of v5, /device:TPU:1, one launch (start us, length us, event | category | flops | bytes accessed | tf_op | source)
XLA Modules:
  0.0 46.8 jit_solution(9261975961012756416)
XLA Ops:
  0.6 0.0 copy-start
  0.6 44.8 %shard_map.120 = (bf16[32,4,8,128]{3,2,1,0:T(8,128)(2,1)S(1)}, f32[8,128,128]{2,1,0:T(8,128)S(1)}, f32[8,128,128]{2,1,0:T(8,128)S(1)}, f32[8,128,128]{2,1,0:T(8,128)S(1)}) custom-call(bf16[4,512,128]{2,1,0:T(8,128)(2,1)} %bitcast.9, bf16[4,512,128]{2,1,0:T(8,128)(2,1)} %bitcast.10, f32[8,128,128]{2,1,0:T(8,128)} %bitcast.11, f32[8,128,128]{2,1,0:T(8,128)} %bitcast.12, ...), custom_call_target="tpu_custom_call" | custom-call | tf_op jit(solution)/shard_map/pallas_call | solution.py:361
  45.4 0.0 copy-done
  45.4 1.4 %shard_map.121 = (bf16[4,512,128]{2,1,0:T(8,128)(2,1)}, f32[8,128,128]{2,1,0:T(8,128)}, f32[8,128,128]{2,1,0:T(8,128)}, f32[8,128,128]{2,1,0:T(8,128)}) custom-call(bf16[32,4,8,128]{3,2,1,0:T(8,128)(2,1)S(1)} %get-tuple-element.12.modes, bf16[512,256]{1,0:T(8,128)(2,1)S(1)} %copy-done, f32[8,128,128]{2,1,0:T(8,128)S(1)} %get-tuple-element.13.new_w, ...), custom_call_target="tpu_custom_call" | custom-call | tf_op jit(solution)/shard_map/pallas_call | solution.py:420
Async XLA Ops:
  0.6 44.8 %copy-start = (bf16[512,256]{1,0:T(8,128)(2,1)S(1)}, bf16[512,256]{1,0:T(8,128)(2,1)}, u32[]{:S(2)}) copy-start(bf16[512,256]{1,0:T(8,128)(2,1)} %constant.11.clone.zy) | copy-start | bytes 786436

commit v6 on v5

--- a/solution.py
+++ b/solution.py
@@ -85,7 +85,8 @@
     yz_hbm,
     fx_hbm,
     bx_hbm,
-    modes,
+    zy_hbm,
+    grad,
     new_w,
     new_first,
     new_second,
@@ -97,6 +98,7 @@
     yz_v,
     fx_v,
     bx_v,
+    zy_v,
     half_v,
     send1,
     recv1,
@@ -106,6 +108,8 @@
     send3,
     recv3,
     send4,
+    modes,
+    part_v,
     in_sem,
     send_sem,
     recv_sem,
@@ -129,16 +133,51 @@
     first_core = core == 0
     second_core = core == 1
     chip = dp - core
-    for k in range(16):
-
-        @pl.when(jnp.logical_or(sp != k, second_core))
-        def _():
-            hello(barrier, chip, k)
-
     gx, gz = dp >> 3, (dp >> 1) & 3
     sy, sz = sp >> 2, sp & 3
+
     mine = dp >> 1
     mx, mz = mine >> 2, mine & 3
+    at_y, at_z = {}, {}
+    for ic in range(2):
+        c = (core + ic) & 1
+        for i in range(4):
+            x = (gx + i) & 3
+            at_y[i, ic] = (x * 8 + c, x * 2 + c, ((mx - x - 2 * c + 8) & 3) * 4)
+            at_z[i, ic] = tri(((1 + 2 * c) * (mz - i + 5)) & 3)
+    samples = [
+        [
+            (at_y[i, ic][0] + 2 * z, at_y[i, ic][1] + 8 * (0, 1, 3, 2)[z], at_y[i, ic][2] + at_z[z, ic])
+            for i in (0, 2, 1, 3)
+            for ic in range(2)
+        ]
+        for z in range(4)
+    ]
+
+    def hello_holders(z):
+        for b, _, s in samples[z][2:]:
+            hello(barrier, b | 1, s)
+        for b, _, s in samples[z][:2]:
+
+            @pl.when(jnp.logical_or(first_core, jnp.logical_or(gz != z, s != sp)))
+            def _():
+                hello(barrier, b | 1, s)
+
+    hello_holders(0)
+    for k in range(16):
+
+        @pl.when(jnp.logical_or(sp != k, second_core))
+        def _():
+            hello(barrier, chip, k)
+
+    for z in range(1, 4):
+        hello_holders(z)
+
+    own_holder = sp < 0
+    for z in range(4):
+        for _, _, s in samples[z][:2]:
+            own_holder = jnp.logical_or(own_holder, jnp.logical_and(gz == z, s == sp))
+
 
     half_way = (sz + 2) & 3
     peer_z = (3 - sz, half_way, 3 - half_way, sz)
@@ -152,33 +191,9 @@
     ]
     my_block = peers[-1][1]
     self_in = my_block == mine
-
-    at_y, at_z, sample = {}, {}, {}
-    for ic in range(2):
-        c = (core + ic) & 1
-        for i in range(4):
-            x, z = (gx + i) & 3, (gz + i) & 3
-            at_y[i, ic] = ((mx - x - 2 * c + 8) & 3) * 4
-            at_z[i, ic] = tri(((1 + 2 * c) * (mz - z + 5)) & 3)
-            sample["x", i] = x * 8
-            sample["z", i] = z * 2
-        sample["c", ic] = c
-    samples = []
-    for iz in (0, 2, 1, 3):
-        for ix in (0, 2, 1, 3):
-            for ic in range(2):
-                b = sample["x", ix] + sample["z", iz] + sample["c", ic]
-                samples.append((b, at_y[ix, ic] + at_z[iz, ic]))
-
-    for b, s in samples[2:]:
-        hello(barrier, b | 1, s)
-    for b, s in samples[:2]:
-
-        @pl.when(jnp.logical_or(first_core, s != sp))
-        def _():
-            hello(barrier, b | 1, s)
-
-    own_holder = jnp.logical_or(samples[0][1] == sp, samples[1][1] == sp)
+    rank = tri(gz)
+    my_slot = rank * 8 + gx * 2 + core
+    batch = (3 + 6 * jnp.minimum(rank, 1) + ((rank + 1) >> 2), 4)
 
     def remote(src, dst, send, recv, b, s):
         pltpu.make_async_remote_copy(
@@ -224,9 +239,11 @@
         b = 2 * my_block + c
         for i in range(1, 16):
             s = (sp + i) & 15
-            remote(send2.at[k, 16 * c + s], recv2.at[k, dp], 3 + k, 3 + k, b, s)
+            remote(send2.at[k, 16 * c + s], recv2.at[k, my_slot], 3 + k, batch[k], b, s)
         here = jnp.logical_and(self_in, core == c)
-        maybe_local(here, send2.at[k, 16 * c + sp], recv2.at[k, dp], 3 + k, 3 + k, b, sp)
+        maybe_local(
+            here, send2.at[k, 16 * c + sp], recv2.at[k, my_slot], 3 + k, batch[k], b, sp
+        )
 
     loads[0].wait()
     loads[1].wait()
@@ -237,6 +254,7 @@
         load(5, bx_hbm, bx_v),
         load(6, first_hbm, first_v),
         load(7, second_hbm, second_v),
+        load(8, zy_hbm, zy_v),
     ]
     yz_modes(0, cot_v)
 
@@ -286,30 +304,44 @@
     send_slab(1, 0, 2)
     send_slab(1, 1, 2)
 
-    arrived(recv2.at[0], 3)
-    cot = recv2[0].astype(F32).reshape(256, C)
-    row = lax.broadcasted_iota(jnp.int32, (256, C), 0)
-    turned = jnp.where(
-        lax.rem(row, 2) == 0, pltpu.roll(cot, 255, 0), -pltpu.roll(cot, 1, 0)
-    )
-    pencil = lax.rem(row // 2, 4)
-    back = jnp.zeros((256, C), F32)
-    for j in range(4):
-        for part, rows in ((0, cot), (1, turned)):
-            g = jnp.where(pencil == j, rows, 0.0).astype(BF16)
-            big_g[:, pl.ds((2 * j + part) * C, C)] = g
-            back += lax.dot_general(
-                g, half_v[2 * j + part], (((1,), (1,)), ((), ())), preferred_element_type=F32
-            )
-    send3[...] = back.astype(BF16).reshape(32, 8, C)
-    for b, s in samples[1:]:
-        remote(send3.at[b], recv3.at[core, sp], 5, 5 + core, b, s)
-    maybe_local(self_in, send3.at[dp], recv3.at[core, sp], 5, 5 + core, *samples[0])
-
+    def mode_grads(first, count):
+        cot = recv2[0, pl.ds(first, count)].astype(F32).reshape(8 * count, C)
+        row = lax.broadcasted_iota(jnp.int32, cot.shape, 0)
+        turned = jnp.where(
+            lax.rem(row, 2) == 0, pltpu.roll(cot, 8 * count - 1, 0), -pltpu.roll(cot, 1, 0)
+        )
+        pencil = lax.rem(row // 2, 4)
+        back = jnp.zeros(cot.shape, F32)
+        for j in range(4):
+            for part, rows in ((0, cot), (1, turned)):
+                g = jnp.where(pencil == j, rows, 0.0).astype(BF16)
+                big_g[pl.ds(8 * first, 8 * count), pl.ds((2 * j + part) * C, C)] = g
+                back += lax.dot_general(
+                    g, half_v[2 * j + part], (((1,), (1,)), ((), ())), preferred_element_type=F32
+                )
+        send3[pl.ds(first, count)] = back.astype(BF16).reshape(count, 8, C)
+
+    def send_grads(z):
+        for b, slot, s in samples[z][1:]:
+            remote(send3.at[slot], recv3.at[core, sp], 5, 5 + core, b, s)
+        b, slot, s = samples[z][0]
+        here = jnp.logical_and(self_in, gz == z)
+        maybe_local(here, send3.at[slot], recv3.at[core, sp], 5, 5 + core, b, s)
+
+    arrived(recv2.at[0, pl.ds(0, 8)], 3)
+    mode_grads(0, 8)
+    send_grads(0)
+    arrived(recv2.at[0, pl.ds(8, 16)], 9)
+    mode_grads(8, 16)
+    send_grads(1)
+    send_grads(3)
     arrived(recv1.at[1], 2)
     for c in range(2):
         x_modes(1, c)
         send_modes(1, c)
+    arrived(recv2.at[0, pl.ds(24, 8)], 10)
+    mode_grads(24, 8)
+    send_grads(2)
 
     loads[5].wait()
     for c in range(2):
@@ -350,18 +382,26 @@
             sent(send2.at[k], 3 + k)
         sent(send3, 5)
 
+    loads[8].wait()
     for c in range(2):
         arrived(modes.at[pl.ds(16 * c, 16)], 7 + c)
-
-
-def exchange(field, cot, weights, first, second, yz, fx, bx):
+        for x in range(4):
+            half = modes[pl.ds(16 * c, 16), x].reshape(128, C)
+            term = dot(zy_v[:, pl.ds(128 * c, 128)], half)
+            if c == 0:
+                part_v[x] = term
+            else:
+                grad[x] = (part_v[x] + term).astype(BF16)
+
+
+def exchange(field, cot, weights, first, second, yz, fx, bx, zy):
     any_spec = pl.BlockSpec(memory_space=pl.ANY)
     vmem_spec = pl.BlockSpec(memory_space=pltpu.VMEM)
     part = pltpu.VMEM((8, C, C), F32)
     return pl.pallas_call(
         kernel,
-        out_shape=(pltpu.VMEM((32, 4, 8, C), BF16), part, part, part),
-        in_specs=[any_spec] * 8,
+        out_shape=(pltpu.VMEM((4, 512, C), BF16), part, part, part),
+        in_specs=[any_spec] * 9,
         out_specs=(vmem_spec,) * 4,
         scratch_shapes=[
             pltpu.VMEM((4, 512, C), BF16),
@@ -372,6 +412,7 @@
             pltpu.VMEM((256, 512), BF16),
             pltpu.VMEM((128, 512), BF16),
             pltpu.VMEM((512, 128), BF16),
+            pltpu.VMEM((512, 256), BF16),
             pltpu.VMEM((8, C, C), BF16),
             pltpu.VMEM((2, 32, 4, 8, C), BF16),
             pltpu.VMEM((2, 32, 4, 8, C), BF16),
@@ -381,50 +422,41 @@
             pltpu.VMEM((32, 8, C), BF16),
             pltpu.VMEM((2, 16, 8, C), BF16),
             pltpu.VMEM((32, 4, 8, C), BF16),
-            pltpu.SemaphoreType.DMA((8,)),
+            pltpu.VMEM((32, 4, 8, C), BF16),
+            pltpu.VMEM((4, 512, C), F32),
             pltpu.SemaphoreType.DMA((9,)),
             pltpu.SemaphoreType.DMA((9,)),
+            pltpu.SemaphoreType.DMA((11,)),
             pltpu.SemaphoreType.REGULAR((2,)),
         ],
         compiler_params=pltpu.CompilerParams(
             collective_id=0, has_side_effects=True, vmem_limit_bytes=VMEM_GRANT
         ),
-    )(field, cot, weights, first, second, yz, fx, bx)
-
-
-def finish_kernel(
-    modes, zy, new_w, new_first, new_second, grad_hbm, w_hbm, first_hbm, second_hbm, grad_v, sem
-):
+    )(field, cot, weights, first, second, yz, fx, bx, zy)
+
+
+def finish_kernel(*refs):
+    sources, targets, sem = refs[:4], refs[4:8], refs[8]
     copies = []
-
-    def store(k, src, dst):
-        copy = pltpu.make_async_copy(src, dst, sem.at[k])
-        copy.start()
-        copies.append(copy)
-
-    store(0, new_w, w_hbm)
-    store(1, new_first, first_hbm)
-    store(2, new_second, second_hbm)
-    for x in range(4):
-        out = dot(zy[...], modes[:, x].reshape(256, C))
-        grad_v[x] = out.astype(BF16)
-        store(3 + x, grad_v.at[x], grad_hbm.at[x])
+    for src, dst in zip(sources, targets, strict=True):
+        rows = src.shape[0] // 4
+        for i in range(4):
+            span = pl.ds(i * rows, rows)
+            copies.append(pltpu.make_async_copy(src.at[span], dst.at[span], sem.at[len(copies)]))
+            copies[-1].start()
     for copy in copies:
         copy.wait()
 
 
-def finish(modes, zy, new_w, new_first, new_second):
-    any_spec = pl.BlockSpec(memory_space=pl.ANY)
-    vmem_spec = pl.BlockSpec(memory_space=pltpu.VMEM)
-    part = jax.ShapeDtypeStruct((8, C, C), F32)
+def finish(*results):
     return pl.pallas_call(
         finish_kernel,
-        out_shape=(jax.ShapeDtypeStruct((4, 512, C), BF16), part, part, part),
-        in_specs=[vmem_spec] * 5,
-        out_specs=(any_spec,) * 4,
-        scratch_shapes=[pltpu.VMEM((4, 512, C), BF16), pltpu.SemaphoreType.DMA((7,))],
+        out_shape=tuple(jax.ShapeDtypeStruct(r.shape, r.dtype) for r in results),
+        in_specs=[pl.BlockSpec(memory_space=pltpu.VMEM)] * 4,
+        out_specs=(pl.BlockSpec(memory_space=pl.ANY),) * 4,
+        scratch_shapes=[pltpu.SemaphoreType.DMA((16,))],
         compiler_params=pltpu.CompilerParams(vmem_limit_bytes=16 * 2**20),
-    )(modes, zy, new_w, new_first, new_second)
+    )(*results)
 
 
 def adam_update(weights, first_moment, second_moment, weight_grads):
@@ -438,7 +470,7 @@
 
 def on_device(field, cotangent, weights, first_moment, second_moment):
     yz, fx, bx, zy = (jnp.asarray(t) for t in tables())
-    modes, new_weights, new_first, new_second = exchange(
+    results = exchange(
         field.reshape(4, 512, C),
         cotangent.reshape(4, 512, C),
         weights.reshape(8, C, C),
@@ -447,8 +479,9 @@
         yz,
         fx,
         bx,
+        zy,
     )
-    field_grad, *state = finish(modes, zy, new_weights, new_first, new_second)
+    field_grad, *state = finish(*results)
     return (field_grad.reshape(field.shape), *(a.reshape(weights.shape) for a in state))
 
 

time: 47.3 us -> 46.9 us (level)
  no operation moved by 1% of the time
where the time goes in v6:
time: 46.9 us; the launch traced here: 46.7 us
  Pallas kernels  46.1 us (98%)
  between operations  0.64 us (1%)
    pallas_call x1, Pallas kernels, exchange(): pl.pallas_call(kernel, out_shape=(pltpu.VMEM((4, 512, C), BF16), part, pa...  44.6 us
    pallas_call x1, Pallas kernels, finish(): pl.pallas_call(finish_kernel, out_shape=tuple((jax.ShapeDtypeStruct(r.sha...  1.44 us

profile of v6, /device:TPU:1, one launch (start us, length us, event | category | flops | bytes accessed | tf_op | source)
XLA Modules:
  0.0 46.7 jit_solution(18353181201554843939)
XLA Ops:
  0.6 44.6 %shard_map.120 = (bf16[4,512,128]{2,1,0:T(8,128)(2,1)S(1)}, f32[8,128,128]{2,1,0:T(8,128)S(1)}, f32[8,128,128]{2,1,0:T(8,128)S(1)}, f32[8,128,128]{2,1,0:T(8,128)S(1)}) custom-call(bf16[4,512,128]{2,1,0:T(8,128)(2,1)} %bitcast.9, bf16[4,512,128]{2,1,0:T(8,128)(2,1)} %bitcast.10, f32[8,128,128]{2,1,0:T(8,128)} %bitcast.11, f32[8,128,128]{2,1,0:T(8,128)} %bitcast.12, ...), custom_call_target="tpu_custom_call" | custom-call | tf_op jit(solution)/shard_map/pallas_call | solution.py:401
  45.3 1.4 %shard_map.121 = (bf16[4,512,128]{2,1,0:T(8,128)(2,1)}, f32[8,128,128]{2,1,0:T(8,128)}, f32[8,128,128]{2,1,0:T(8,128)}, f32[8,128,128]{2,1,0:T(8,128)}) custom-call(bf16[4,512,128]{2,1,0:T(8,128)(2,1)S(1)} %get-tuple-element.12.refs_0_, f32[8,128,128]{2,1,0:T(8,128)S(1)} %get-tuple-element.13.refs_1_, f32[8,128,128]{2,1,0:T(8,128)S(1)} %get-tuple-element.14.refs_2_, ...), custom_call_target="tpu_custom_call" | custom-call | tf_op jit(solution)/shard_map/pallas_call | solution.py:452

commit v7 on v6

--- a/solution.py
+++ b/solution.py
@@ -289,8 +289,18 @@
 
         hello(met.at[1], chip, sp)
 
+    def second_chunk():
+        arrived(recv1.at[0, pl.ds(16, 16)], 1)
+        x_modes(0, 1)
+
     arrived(recv1.at[0, pl.ds(0, 16)], 0)
     x_modes(0, 0)
+
+    both_first = jnp.logical_and(gz == 0, first_core)
+
+    @pl.when(both_first)
+    def _():
+        second_chunk()
 
     @pl.when(first_core)
     def _():
@@ -298,8 +308,11 @@
             pl.semaphore_wait(met.at[1], 1)
 
     send_modes(0, 0)
-    arrived(recv1.at[0, pl.ds(16, 16)], 1)
-    x_modes(0, 1)
+
+    @pl.when(jnp.logical_not(both_first))
+    def _():
+        second_chunk()
+
     send_modes(0, 1)
     send_slab(1, 0, 2)
     send_slab(1, 1, 2)

time: 46.9 us -> 46.5 us (level)
  Pallas kernels: 46.1 us -> 45.6 us
    pallas_call x1, Pallas kernels: 44.6 us -> 44.2 us  [exchange(): pl.pallas_call(kernel, out_shape=(pltpu.VMEM((4, 512, C), BF16), part, pa...]
where the time goes in v7:
time: 46.5 us; the launch traced here: 46.2 us
  Pallas kernels  45.6 us (98%)
  between operations  0.64 us (1%)
    pallas_call x1, Pallas kernels, exchange(): pl.pallas_call(kernel, out_shape=(pltpu.VMEM((4, 512, C), BF16), part, pa...  44.2 us
    pallas_call x1, Pallas kernels, finish(): pl.pallas_call(finish_kernel, out_shape=tuple((jax.ShapeDtypeStruct(r.sha...  1.44 us

profile of v7, /device:TPU:1, one launch (start us, length us, event | category | flops | bytes accessed | tf_op | source)
XLA Modules:
  0.0 46.2 jit_solution(13620120946501200177)
XLA Ops:
  0.6 44.2 %shard_map.120 = (bf16[4,512,128]{2,1,0:T(8,128)(2,1)S(1)}, f32[8,128,128]{2,1,0:T(8,128)S(1)}, f32[8,128,128]{2,1,0:T(8,128)S(1)}, f32[8,128,128]{2,1,0:T(8,128)S(1)}) custom-call(bf16[4,512,128]{2,1,0:T(8,128)(2,1)} %bitcast.9, bf16[4,512,128]{2,1,0:T(8,128)(2,1)} %bitcast.10, f32[8,128,128]{2,1,0:T(8,128)} %bitcast.11, f32[8,128,128]{2,1,0:T(8,128)} %bitcast.12, ...), custom_call_target="tpu_custom_call" | custom-call | tf_op jit(solution)/shard_map/pallas_call | solution.py:414
  44.8 1.4 %shard_map.121 = (bf16[4,512,128]{2,1,0:T(8,128)(2,1)}, f32[8,128,128]{2,1,0:T(8,128)}, f32[8,128,128]{2,1,0:T(8,128)}, f32[8,128,128]{2,1,0:T(8,128)}) custom-call(bf16[4,512,128]{2,1,0:T(8,128)(2,1)S(1)} %get-tuple-element.12.refs_0_, f32[8,128,128]{2,1,0:T(8,128)S(1)} %get-tuple-element.13.refs_1_, f32[8,128,128]{2,1,0:T(8,128)S(1)} %get-tuple-element.14.refs_2_, ...), custom_call_target="tpu_custom_call" | custom-call | tf_op jit(solution)/shard_map/pallas_call | solution.py:465
